TPU v7x, 128 devices: a whole 4x4x4 slice. The times are simulated.
128 devices in a mesh: chan: 8 (over y, core), inp: 16 (over z, x).
Axes of the slice: x: 4, y: 4, z: 4, core: 2. Of those that a mesh axis runs over, the one named last changes fastest.
Arguments:
- voltages: bfloat16 [1024, 262144], P('inp', 'chan'), may hold values from -64 to 64
- tile_table: int32 [144, 2], replicated, may hold values from -1 to 15, as said below
Outputs:
- coherence: float32 [512, 144, 64, 128], P('chan', 'inp')
Inputs may be any that keep to these rules, and one draw needn't show every extreme that they name: `tile_table`: rows 9 d to 9 d + 8 are the slots whose tiles the device at index d along inp outputs. Every pair (a, b) with 0 <= a <= b < 16 stands in exactly one row, and every other row is (-1, -1); the pairs are spread over the rows in any order.
All inputs are finite; a program needn't handle non-finite values.
Results may differ from a plain program's by a relative error of at most 0.0058.
Values may be sent and summed in bfloat16 or wider, within the bound.
No kernel may reach another device: no remote copies, remote signals or barrier semaphores. Data moves between devices by JAX's collectives and lax.ppermute only.
A program may use at most 128 MiB of HBM per device.

v0:
```python
import math

import jax
import jax.numpy as jnp
from jax import lax
from jax.sharding import Mesh
from jax.sharding import PartitionSpec as P

L = 2048
NCH = 512
TAPS = 4
CHAN = ("chan_0", "chan_1")


def passed_along(array, axis, by):
    devices = lax.axis_size(axis)
    pairs = [(i, i + by) for i in range(devices) if 0 <= i + by < devices]
    return lax.ppermute(array, axis, pairs)


def in_blocks(array, dim, devices):
    before, after = (array.shape[:dim], array.shape[dim + 1 :])
    return jnp.moveaxis(array.reshape(*before, devices, -1, *after), dim, 0)


def laid_out(parts, dim):
    parts = jnp.moveaxis(parts, 0, dim)
    shape = parts.shape
    return parts.reshape(*shape[:dim], shape[dim] * shape[dim + 1], *shape[dim + 2 :])


def exchange_in_order(parts, axes, order):
    inside = parts.shape[1:]
    whole = parts.reshape(*(lax.axis_size(a) for a in axes), *inside)
    for k in order:
        whole = lax.all_to_all(whole, axes[k], k, k, tiled=True)
    return whole.reshape(-1, *inside)


def core_and_chips(array, groups, order, split_dim, concat_dim):
    devices = lax.axis_size(groups[0]) * lax.axis_size(groups[1])
    parts = in_blocks(array, split_dim, devices)
    return laid_out(exchange_in_order(parts, groups, order), concat_dim)


def filter_window():
    positions = jnp.arange(TAPS * L, dtype=jnp.float32)
    shape_sinc = jnp.sinc((positions - TAPS * L / 2.0) / L)
    tapering = 0.5 - 0.5 * jnp.cos(2.0 * math.pi * positions / (TAPS * L))
    return (shape_sinc * tapering).reshape(TAPS, L)


def transform_table():
    samples = jnp.arange(L, dtype=jnp.int32)[:, None]
    channels = jnp.arange(NCH, dtype=jnp.int32)[None, :]
    phases = samples * channels % L
    angles = phases.astype(jnp.float32) * (2.0 * math.pi / L)
    return (
        jnp.stack([jnp.cos(angles), -jnp.sin(angles)], axis=2)
        .reshape(L, 2 * NCH)
        .astype(jnp.bfloat16)
    )


def rotate_parts(rows):
    half_width = rows.shape[-1] // 2
    return jnp.concatenate([-rows[..., half_width:], rows[..., :half_width]], axis=-1)


def arrange(turned):
    input_count, frame_total, column_count = turned.shape
    return (
        turned.reshape(input_count, frame_total, column_count // 2, 2)
        .transpose(2, 0, 3, 1)
        .reshape(column_count // 2, input_count, 2 * frame_total)
    )


def channelize(voltages):
    block_width, local_len = voltages.shape
    local_frames = local_len // L
    blocks = voltages.reshape(block_width, local_frames, L)
    following = passed_along(blocks[:, : TAPS - 1, :], CHAN, -1)
    extended = jnp.concatenate([blocks, following], axis=1)
    window = filter_window()
    filtered = jnp.zeros((block_width, local_frames, L), jnp.float32)
    for tap_index in range(TAPS):
        filtered = (
            filtered
            + extended[:, tap_index : tap_index + local_frames, :].astype(jnp.float32)
            * window[tap_index]
        )
    filtered = filtered.astype(jnp.bfloat16).reshape(block_width * local_frames, L)
    spectra = jnp.dot(filtered, transform_table(), preferred_element_type=jnp.float32).astype(
        jnp.bfloat16
    )
    return spectra.reshape(block_width, local_frames, 2 * NCH)


def make_tile(everything, autopower, row_block, col_block, block_width, frame_total):
    present = (row_block >= 0).astype(jnp.float32)
    first = jnp.maximum(row_block, 0)
    second = jnp.maximum(col_block, 0)
    left_rows = lax.dynamic_slice_in_dim(everything, first * block_width, block_width, 1)
    right_rows = lax.dynamic_slice_in_dim(everything, second * block_width, block_width, 1)
    partner = jnp.concatenate([right_rows, rotate_parts(right_rows)], axis=1)
    product = jnp.einsum("cif,cjf->cij", left_rows, partner, preferred_element_type=jnp.float32)
    power_left = lax.dynamic_slice_in_dim(autopower, first * block_width, block_width, 1)
    power_right = lax.dynamic_slice_in_dim(autopower, second * block_width, block_width, 1)
    inverse = present / (frame_total * jnp.sqrt(power_left[:, :, None] * power_right[:, None, :]))
    return product * jnp.concatenate([inverse, inverse], axis=2)


def on_device(voltages, tile_table):
    block_width = voltages.shape[0]
    spectra = channelize(voltages)
    turned = core_and_chips(spectra, ("chan_0", "chan_1"), (1, 0), 2, 1)
    own = arrange(turned)
    everything = lax.all_gather(own, "inp", axis=1, tiled=True)
    frame_total = everything.shape[2] // 2
    autopower = jnp.sum(jnp.square(everything.astype(jnp.float32)), axis=2) / frame_total + 1e-06
    slot_total = tile_table.shape[0] // lax.axis_size("inp")
    device_index = lax.axis_index("inp")
    slot_rows = lax.dynamic_slice_in_dim(tile_table, device_index * slot_total, slot_total, 0)
    outputs = jnp.zeros(
        (everything.shape[0], slot_total, block_width, 2 * block_width), jnp.float32
    )

    def place(slot_index, current):
        tile_out = make_tile(
            everything,
            autopower,
            slot_rows[slot_index, 0],
            slot_rows[slot_index, 1],
            block_width,
            frame_total,
        )
        return lax.dynamic_update_index_in_dim(current, tile_out, slot_index, 1)

    return lax.fori_loop(0, slot_total, place, outputs)


def solution(mesh):
    torus = Mesh(mesh.devices.reshape(4, 2, mesh.shape["inp"]), ("chan_0", "chan_1", "inp"))
    placed = (P("inp", CHAN), P())
    return jax.shard_map(
        on_device,
        mesh=torus,
        in_specs=placed,
        out_specs=P(CHAN, "inp", None, None),
        check_vma=False,
    )
```

profile of v0, /device:TPU:0, one launch (start us, length us, event | category | flops | bytes accessed | tf_op | source)
XLA Modules:
  0.0 442.8 jit_solution(10876512019919204436)
XLA Ops:
  6.5 4.6 %copy.31 = bf16[8,8,16,2048]{3,2,1,0:T(8,128)(2,1)S(1)} copy(bf16[8,8,16,2048]{3,1,2,0:T(8,128)(2,1)} %bitcast.47) | data formatting | bytes 8388608
  11.2 2.0 copy-done.2
  14.3 1.5 collective-permute-start
  15.8 17.1 %negate_convert_fusion = (bf16[2048,512,1]{1,0,2:T(8,128)(2,1)S(1)}, bf16[2048,512,1]{1,0,2:T(8,128)(2,1)S(1)}) fusion(), kind=kLoop, calls=%fused_computation.29 | loop fusion | flops 17825792 | bytes 4194304 | tf_op jit(solution)/shard_map/convert.2
  32.9 2.3 pad_maximum_fusion
  35.2 11.3 %copy.21 = bf16[2048,512,2]{0,2,1:T(2,128)(2,1)} copy(bf16[2048,512,2]{1,0,2:T(8,128)(2,1)} %pad_maximum_fusion) | data formatting | bytes 8388608 | tf_op jit(solution)/shard_map/stack | solution.py:59
  46.6 7.3 %convert_element_type.68 = bf16[2048,1024]{0,1:T(8,128)(2,1)} reshape(bf16[2048,512,2]{0,2,1:T(2,128)(2,1)} %copy.21) | data formatting | bytes 8388608 | tf_op jit(solution)/shard_map/convert_element_type | solution.py:61
  54.0 2.7 constant_dynamic-update-slice_fusion
  56.7 1.0 copy_dynamic-update-slice_fusion
  57.8 5.0 %add_convert_fusion = bf16[64,16,2048]{2,1,0:T(8,128)(2,1)S(1)} fusion(bf16[64,19,2048]{2,1,0:T(8,128)(2,1)S(1)} %copy_dynamic-update-slice_fusion, f32[2048]{0:T(1024)S(1)} %get-tuple-element.117, f32[2048]{0:T(1024)S(1)} %get-tuple-element.118, f32[2048]{0:T(1024)S(1)} %get-tuple-element.119, f32[2048]{0:T(1024)S(1)} %get-tuple-element.116, ...), kind=kLoop, calls=%fused_computation.21 | loop fusion | flops 25165824 | bytes 21004288 | tf_op jit(solution)/shard_map/convert_element_type | solution.py:93
  62.7 4.8 %convert_bitcast_fusion = bf16[128,8,8,128]{3,1,2,0:T(8,128)(2,1)S(1)} fusion(bf16[1024,2048]{1,0:T(8,128)(2,1)S(1)} %bitcast.46, bf16[2048,1024]{0,1:T(8,128)(2,1)S(1)} %copy-done.4), kind=kOutput, calls=%fused_computation.34 | convolution fusion | flops 4296015872 | bytes 10485760 | tf_op jit(solution)/shard_map/dot_general | solution.py:94
  67.5 0.6 copy.32
  68.8 6.0 %all_to_all.10 = bf16[4,2,64,16,128]{4,3,2,0,1:T(8,128)(2,1)S(1)} all-to-all(bf16[4,2,64,16,128]{4,3,2,0,1:T(8,128)(2,1)S(1)} %copy.23), channel_id=1, replica_groups=mesh['chan_0'=4,'chan_1'=2,'inp'=16] {'chan_1'}, dimensions={1} | all-to-all | bytes 4194304 | tf_op jit(solution)/shard_map/all_to_all | solution.py:36
  75.2 31.0 %all_to_all.11 = bf16[4,2,64,16,128]{4,3,2,1,0:T(8,128)(2,1)S(1)} all-to-all(bf16[4,2,64,16,128]{4,3,2,1,0:T(8,128)(2,1)S(1)} %copy.24), channel_id=1, replica_groups=mesh['chan_0'=4,'chan_1'=2,'inp'=16] {'chan_0'}, dimensions={0} | all-to-all | bytes 4194304 | tf_op jit(solution)/shard_map/all_to_all | solution.py:36
  106.2 7.4 %copy.25 = bf16[8,64,16,128]{1,2,0,3:T(8,128)(2,1)} copy(bf16[8,64,16,128]{3,2,1,0:T(8,128)(2,1)S(1)} %bitcast.43) | data formatting | bytes 4194304 | tf_op jit(solution)/shard_map/reshape | solution.py:37
  113.6 4.8 %copy.26 = bf16[64,64,256]{2,1,0:T(8,128)(2,1)} copy(bf16[64,64,256]{1,2,0:T(8,128)(2,1)} %bitcast.42) | data formatting | bytes 4194304 | tf_op jit(solution)/shard_map/reshape | solution.py:75
  118.5 197.5 %all-gather.2.cloned.1.call-done = bf16[64,1024,256]{2,1,0:T(8,128)(2,1)} async-done(((bf16[64,64,256]{2,1,0:T(8,128)(2,1)}), bf16[64,1024,256]{2,1,0:T(8,128)(2,1)}) %all-gather.2.cloned.1.call-update) | async-done | bytes 33554448 | tf_op jit(solution)/shard_map/all_gather | solution.py:119
  316.0 11.9 %multiply_reduce_fusion = f32[64,1024]{1,0:T(8,128)S(1)} fusion(bf16[64,1024,256]{2,1,0:T(8,128)(2,1)} %all-gather.2.cloned.1.call-done), kind=kLoop, calls=%fused_computation.20 | loop fusion | flops 50266112 | bytes 33816576 | tf_op jit(solution)/shard_map/reduce_sum | solution.py:121
  327.9 107.4 %while.13 = (s32[]{:T(128)}, f32[64,9,64,128]{3,2,1,0:T(8,128)}, s32[9,2]{0,1:T(2,128)S(1)}, bf16[64,1024,256]{2,1,0:T(8,128)(2,1)}, f32[64,1024]{1,0:T(8,128)S(...) while((s32[]{:T(128)}, f32[64,9,64,128]{3,2,1,0:T(8,128)}, ...), condition=%wide.region_2.3_spmd, body=%wide.region_1.2_spmd.sunk | while | flops 284426240 | bytes 18973484 | solution.py:140
  327.9 0.6 constant_dynamic-slice_fusion.10
  330.5 0.8 multiply_divide_fusion.2
  331.4 2.1 dynamic-slice_negate_fusion.2
  333.5 1.7 constant_dynamic-slice_fusion.12
  335.2 4.6 %fusion.57 = f32[64,9,64,128]{3,2,1,0:T(8,128)} fusion(f32[64,9,64,128]{3,2,1,0:T(8,128)} %get-tuple-element.177, s32[]{:T(128)} %get-tuple-element.176, f32[64,64,64]{2,1,0:T(8,128)S(1)} %multiply_divide_fusion.2, bf16[64,64,128]{2,1,0:T(8,128)(2,1)S(1)} %get-tuple-element.163, bf16[64,64,128]{2,1,0:T(8,128)(2,1)S(1)} %get-tuple-element.164, ...), kind=kOutput, calls=%fused_computation.8.clone.1 | convolution fusion | flops 282066944 | bytes 9437700 | tf_op jit(solution)/shard_map/while/body/eval_jaxpr/cif,cjf->cij/dot_general | solution.py:107
  339.8 0.6 constant_dynamic-slice_fusion.10
  342.5 0.8 multiply_divide_fusion.2
  343.3 2.1 dynamic-slice_negate_fusion.2
  345.4 1.7 constant_dynamic-slice_fusion.12
  347.2 4.6 %fusion.57 = f32[64,9,64,128]{3,2,1,0:T(8,128)} fusion(f32[64,9,64,128]{3,2,1,0:T(8,128)} %get-tuple-element.177, s32[]{:T(128)} %get-tuple-element.176, f32[64,64,64]{2,1,0:T(8,128)S(1)} %multiply_divide_fusion.2, bf16[64,64,128]{2,1,0:T(8,128)(2,1)S(1)} %get-tuple-element.163, bf16[64,64,128]{2,1,0:T(8,128)(2,1)S(1)} %get-tuple-element.164, ...), kind=kOutput, calls=%fused_computation.8.clone.1 | convolution fusion | flops 282066944 | bytes 9437700 | tf_op jit(solution)/shard_map/while/body/eval_jaxpr/cif,cjf->cij/dot_general | solution.py:107
  351.8 0.6 constant_dynamic-slice_fusion.10
  354.4 0.8 multiply_divide_fusion.2
  355.2 2.1 dynamic-slice_negate_fusion.2
  357.3 1.7 constant_dynamic-slice_fusion.12
  359.1 4.6 %fusion.57 = f32[64,9,64,128]{3,2,1,0:T(8,128)} fusion(f32[64,9,64,128]{3,2,1,0:T(8,128)} %get-tuple-element.177, s32[]{:T(128)} %get-tuple-element.176, f32[64,64,64]{2,1,0:T(8,128)S(1)} %multiply_divide_fusion.2, bf16[64,64,128]{2,1,0:T(8,128)(2,1)S(1)} %get-tuple-element.163, bf16[64,64,128]{2,1,0:T(8,128)(2,1)S(1)} %get-tuple-element.164, ...), kind=kOutput, calls=%fused_computation.8.clone.1 | convolution fusion | flops 282066944 | bytes 9437700 | tf_op jit(solution)/shard_map/while/body/eval_jaxpr/cif,cjf->cij/dot_general | solution.py:107
  363.7 0.6 constant_dynamic-slice_fusion.10
  366.3 0.8 multiply_divide_fusion.2
  367.2 2.1 dynamic-slice_negate_fusion.2
  369.3 1.7 constant_dynamic-slice_fusion.12
  371.0 4.6 %fusion.57 = f32[64,9,64,128]{3,2,1,0:T(8,128)} fusion(f32[64,9,64,128]{3,2,1,0:T(8,128)} %get-tuple-element.177, s32[]{:T(128)} %get-tuple-element.176, f32[64,64,64]{2,1,0:T(8,128)S(1)} %multiply_divide_fusion.2, bf16[64,64,128]{2,1,0:T(8,128)(2,1)S(1)} %get-tuple-element.163, bf16[64,64,128]{2,1,0:T(8,128)(2,1)S(1)} %get-tuple-element.164, ...), kind=kOutput, calls=%fused_computation.8.clone.1 | convolution fusion | flops 282066944 | bytes 9437700 | tf_op jit(solution)/shard_map/while/body/eval_jaxpr/cif,cjf->cij/dot_general | solution.py:107
  375.6 0.6 constant_dynamic-slice_fusion.10
  378.3 0.8 multiply_divide_fusion.2
  379.1 2.1 dynamic-slice_negate_fusion.2
  381.2 1.7 constant_dynamic-slice_fusion.12
  382.9 4.6 %fusion.57 = f32[64,9,64,128]{3,2,1,0:T(8,128)} fusion(f32[64,9,64,128]{3,2,1,0:T(8,128)} %get-tuple-element.177, s32[]{:T(128)} %get-tuple-element.176, f32[64,64,64]{2,1,0:T(8,128)S(1)} %multiply_divide_fusion.2, bf16[64,64,128]{2,1,0:T(8,128)(2,1)S(1)} %get-tuple-element.163, bf16[64,64,128]{2,1,0:T(8,128)(2,1)S(1)} %get-tuple-element.164, ...), kind=kOutput, calls=%fused_computation.8.clone.1 | convolution fusion | flops 282066944 | bytes 9437700 | tf_op jit(solution)/shard_map/while/body/eval_jaxpr/cif,cjf->cij/dot_general | solution.py:107
  387.6 0.6 constant_dynamic-slice_fusion.10
  390.2 0.8 multiply_divide_fusion.2
  391.0 2.1 dynamic-slice_negate_fusion.2
  393.1 1.7 constant_dynamic-slice_fusion.12
  394.9 4.6 %fusion.57 = f32[64,9,64,128]{3,2,1,0:T(8,128)} fusion(f32[64,9,64,128]{3,2,1,0:T(8,128)} %get-tuple-element.177, s32[]{:T(128)} %get-tuple-element.176, f32[64,64,64]{2,1,0:T(8,128)S(1)} %multiply_divide_fusion.2, bf16[64,64,128]{2,1,0:T(8,128)(2,1)S(1)} %get-tuple-element.163, bf16[64,64,128]{2,1,0:T(8,128)(2,1)S(1)} %get-tuple-element.164, ...), kind=kOutput, calls=%fused_computation.8.clone.1 | convolution fusion | flops 282066944 | bytes 9437700 | tf_op jit(solution)/shard_map/while/body/eval_jaxpr/cif,cjf->cij/dot_general | solution.py:107
  399.5 0.6 constant_dynamic-slice_fusion.10
  402.1 0.8 multiply_divide_fusion.2
  403.0 2.1 dynamic-slice_negate_fusion.2
  405.1 1.7 constant_dynamic-slice_fusion.12
  406.8 4.6 %fusion.57 = f32[64,9,64,128]{3,2,1,0:T(8,128)} fusion(f32[64,9,64,128]{3,2,1,0:T(8,128)} %get-tuple-element.177, s32[]{:T(128)} %get-tuple-element.176, f32[64,64,64]{2,1,0:T(8,128)S(1)} %multiply_divide_fusion.2, bf16[64,64,128]{2,1,0:T(8,128)(2,1)S(1)} %get-tuple-element.163, bf16[64,64,128]{2,1,0:T(8,128)(2,1)S(1)} %get-tuple-element.164, ...), kind=kOutput, calls=%fused_computation.8.clone.1 | convolution fusion | flops 282066944 | bytes 9437700 | tf_op jit(solution)/shard_map/while/body/eval_jaxpr/cif,cjf->cij/dot_general | solution.py:107
  411.4 0.6 constant_dynamic-slice_fusion.10
  414.1 0.8 multiply_divide_fusion.2
  414.9 2.1 dynamic-slice_negate_fusion.2
  417.0 1.7 constant_dynamic-slice_fusion.12
  418.7 4.6 %fusion.57 = f32[64,9,64,128]{3,2,1,0:T(8,128)} fusion(f32[64,9,64,128]{3,2,1,0:T(8,128)} %get-tuple-element.177, s32[]{:T(128)} %get-tuple-element.176, f32[64,64,64]{2,1,0:T(8,128)S(1)} %multiply_divide_fusion.2, bf16[64,64,128]{2,1,0:T(8,128)(2,1)S(1)} %get-tuple-element.163, bf16[64,64,128]{2,1,0:T(8,128)(2,1)S(1)} %get-tuple-element.164, ...), kind=kOutput, calls=%fused_computation.8.clone.1 | convolution fusion | flops 282066944 | bytes 9437700 | tf_op jit(solution)/shard_map/while/body/eval_jaxpr/cif,cjf->cij/dot_general | solution.py:107
  426.0 0.8 multiply_divide_fusion.2
  426.8 2.1 dynamic-slice_negate_fusion.2
  428.9 1.7 constant_dynamic-slice_fusion.12
  430.7 4.6 %fusion.57 = f32[64,9,64,128]{3,2,1,0:T(8,128)} fusion(f32[64,9,64,128]{3,2,1,0:T(8,128)} %get-tuple-element.177, s32[]{:T(128)} %get-tuple-element.176, f32[64,64,64]{2,1,0:T(8,128)S(1)} %multiply_divide_fusion.2, bf16[64,64,128]{2,1,0:T(8,128)(2,1)S(1)} %get-tuple-element.163, bf16[64,64,128]{2,1,0:T(8,128)(2,1)S(1)} %get-tuple-element.164, ...), kind=kOutput, calls=%fused_computation.8.clone.1 | convolution fusion | flops 282066944 | bytes 9437700 | tf_op jit(solution)/shard_map/while/body/eval_jaxpr/cif,cjf->cij/dot_general | solution.py:107
  435.3 0.7 copy-done.1
  (31 shorter events, 3.9 us)
Async XLA Ops:
  6.5 111.8 %copy-start = (s32[144,2]{0,1:T(2,128)S(1)}, s32[144,2]{0,1:T(2,128)}, u32[]{:S(2)}) copy-start(s32[144,2]{0,1:T(2,128)} %param.5) | copy-start | bytes 3460
  6.5 309.4 %all-gather.2.cloned.1.call-start = ((), (), s32[]{:S(2)}) async-start(), calls=%async_computation.2 | async-start | bytes 35651584 | tf_op jit(solution)/shard_map/all_gather | solution.py:119
  11.1 2.0 copy-start.2
  14.3 42.4 %collective-permute-start = (bf16[64,3,2048]{2,0,1:T(8,128)(2,1)S(1)}, bf16[64,3,2048]{2,0,1:T(8,128)(2,1)S(1)}, u32[]{:S(2)}, u32[]{:S(2)}) collective-permute-start(bf16[64,3,2048]{2,0,1:T(8,128)(2,1)S(1)} %copy.19), channel_id=1, source_target_pairs={{16,0},{32,16},{48,32},{64,48},{80,64},{96,80},{112,96},{17,1},{33... | collective-permute-start | bytes 2359304 | tf_op jit(solution)/shard_map/ppermute | solution.py:18
  54.0 3.7 copy-start.3
  57.8 5.0 %copy-start.4 = (bf16[2048,1024]{0,1:T(8,128)(2,1)S(1)}, bf16[2048,1024]{0,1:T(8,128)(2,1)}, u32[]{:S(2)}) copy-start(bf16[2048,1024]{0,1:T(8,128)(2,1)} %convert_element_type.68) | copy-start | bytes 12582916
  435.3 0.7 copy-start.1
Sparse Core Ops, SparseCore 0:
  118.5 197.4 all-gather.1
where the time goes:
time: 445 us; the launch traced here: 443 us
  waiting for transfers between devices  198 us (44%)
  local copies, waits for them, and re-layouts  66.6 us (15%)
  other arithmetic  62.7 us (14%)
  matrix products  46.3 us (10%)
  blocking collectives  37.1 us (8%)
  loops' own time  17.5 us (4%)
  between operations  13.6 us (3%)
    all_gather x1, waiting for transfers between devices, on_device(): everything = lax.all_gather(own, 'inp', axis=1, tiled=True)  198 us
    dot_general x9, matrix products, make_tile(): jnp.einsum('cif,cjf->cij', left_rows, partner, preferred_element_type=jnp...  41.6 us
    all_to_all x2, blocking collectives, exchange_in_order(): whole = lax.all_to_all(whole, axes[k], k, k, tiled=True)  37.1 us
    neg x9, other arithmetic, rotate_parts(): -rows[..., half_width:]  18.8 us
    another operation x1, loops' own time, on_device(): return lax.fori_loop(0, slot_total, place, outputs)  17.5 us
    another operation x1, other arithmetic  17.1 us
    dynamic_slice x9, local copies, waits for them, and re-layouts, make_tile(): lax.dynamic_slice_in_dim(everything, second * block_width, block_width, 1)  15.7 us
    reduce_sum x1, other arithmetic, on_device(): jnp.sum(jnp.square(everything.astype(jnp.float32)), axis=2) / frame_total  11.9 us
  transfers between devices with their start and end apart: 2, of which 1 were waited for; matrix products, arithmetic and copies ran while one was open for 9% of the time, Pallas kernels for 0%

commit v1 on v0

v1 whole, which is shorter than its diff:
```python
import math

import jax
import jax.numpy as jnp
import numpy as np
from jax import lax
from jax.experimental import pallas as pl
from jax.experimental.pallas import tpu as pltpu
from jax.sharding import PartitionSpec as P

L = 2048
NCH = 512
TAPS = 4
LANES = 128
STEP = 4
COARSE = 16
EVERY = ("chan", "inp")


def filter_window():
    positions = np.arange(TAPS * L, dtype=np.float64)
    tapering = 0.5 - 0.5 * np.cos(2.0 * math.pi * positions / (TAPS * L))
    shape_sinc = np.sinc((positions - TAPS * L / 2.0) / L)
    return (shape_sinc * tapering).reshape(TAPS, L).astype(np.float32)


def twiddle_factors():
    samples = np.arange(L)[None, :]
    coarse = (COARSE * np.arange(NCH // COARSE)[:, None] * samples) % L
    rows = np.arange(2 * COARSE)[:, None]
    fine = ((rows // 2) * samples + (rows % 2) * (L // 4)) % L
    unit = 2.0 * math.pi / L
    tables = [np.cos(coarse * unit), np.sin(coarse * unit), np.cos(fine * unit), np.sin(fine * unit)]
    return [t.astype(np.float32) for t in tables]


def build_table(coarse_cos, coarse_sin, fine_cos, fine_sin, table):
    rows = 2 * COARSE

    def column(j, carry):
        lanes = pl.ds(pl.multiple_of(j * LANES, LANES), LANES)
        fc = fine_cos[:, lanes]
        fs = fine_sin[:, lanes]
        for a in range(NCH // COARSE):
            part = coarse_cos[a : a + 1, lanes] * fc - coarse_sin[a : a + 1, lanes] * fs
            table[a * rows : (a + 1) * rows, lanes] = part.astype(jnp.bfloat16)
        return carry

    lax.fori_loop(0, L // LANES, column, 0)


def filter_frames(window, current, following, filtered):
    width = current.shape[0]

    def column(j, carry):
        taps = [window[k : k + 1, pl.ds(pl.multiple_of(j * LANES, LANES), LANES)] for k in range(TAPS)]
        for r in range(0, width, 16):
            rows = slice(r, r + 16)
            frames = []
            for f in range(STEP + TAPS - 1):
                source, at = (current, f) if f < STEP else (following, f - STEP)
                lanes = pl.ds(pl.multiple_of(j * LANES + at * L, LANES), LANES)
                frames.append(source[rows, lanes].astype(jnp.float32))
            for f in range(STEP):
                total = frames[f] * taps[0]
                for k in range(1, TAPS):
                    total = total + frames[f + k] * taps[k]
                filtered[f * width + r : f * width + r + 16, pl.ds(pl.multiple_of(j * LANES, LANES), LANES)] = (
                    total.astype(jnp.bfloat16)
                )
        return carry

    lax.fori_loop(0, L // LANES, column, 0)


def transform(table, filtered, spectra):
    rows = 256

    def chunk(i, carry):
        at = pl.ds(pl.multiple_of(i * rows, rows), rows)
        product = lax.dot_general(
            table[at, :], filtered[...], (((1,), (1,)), ((), ())), preferred_element_type=jnp.float32
        )
        spectra[at, :] = product.astype(jnp.bfloat16)
        return carry

    lax.fori_loop(0, 2 * NCH // rows, chunk, 0)


def early_kernel(cc, cs, fc, fs, window, current, following, spectra, table, filtered):
    @pl.when(pl.program_id(0) == 0)
    def _():
        build_table(cc, cs, fc, fs, table)

    filter_frames(window, current, following, filtered)
    transform(table, filtered, spectra)


def late_kernel(table, window, current, following, earlier, spectra, filtered):
    del earlier
    filter_frames(window, current, following, filtered)
    transform(table, filtered, spectra)


def channelize(voltages):
    width, local_len = voltages.shape
    steps = local_len // (STEP * L)
    span = STEP * L
    halo = (TAPS - 1) * L
    devices = lax.axis_size("chan")
    following = lax.ppermute(voltages[:, :halo], "chan", [(i, i - 1) for i in range(1, devices)])
    window = jnp.asarray(filter_window())
    factors = [jnp.asarray(t) for t in twiddle_factors()]
    columns = STEP * width
    whole = lambda shape: pl.BlockSpec(shape, lambda *_: (0, 0))
    spectra_shape = jax.ShapeDtypeStruct((2 * NCH, steps * columns), jnp.bfloat16)
    early, table = pl.pallas_call(
        early_kernel,
        name="channelize_early",
        grid=(steps - 1,),
        in_specs=[whole(t.shape) for t in factors]
        + [
            whole((TAPS, L)),
            pl.BlockSpec((width, span), lambda j: (0, j)),
            pl.BlockSpec((width, span), lambda j: (0, j + 1)),
        ],
        out_specs=[pl.BlockSpec((2 * NCH, columns), lambda j: (0, j)), whole((2 * NCH, L))],
        out_shape=[spectra_shape, jax.ShapeDtypeStruct((2 * NCH, L), jnp.bfloat16)],
        scratch_shapes=[pltpu.VMEM((columns, L), jnp.bfloat16)],
        cost_estimate=pl.CostEstimate(flops=3 * 10**9, bytes_accessed=12 * 2**20, transcendentals=0),
    )(*factors, window, voltages, voltages)
    return pl.pallas_call(
        late_kernel,
        name="channelize_late",
        grid=(1,),
        in_specs=[
            whole((2 * NCH, L)),
            whole((TAPS, L)),
            pl.BlockSpec((width, span), lambda j: (0, steps - 1)),
            whole((width, halo)),
            pl.BlockSpec(memory_space=pl.ANY),
        ],
        out_specs=pl.BlockSpec((2 * NCH, columns), lambda j: (0, steps - 1)),
        out_shape=spectra_shape,
        scratch_shapes=[pltpu.VMEM((columns, L), jnp.bfloat16)],
        input_output_aliases={4: 0},
        cost_estimate=pl.CostEstimate(flops=10**9, bytes_accessed=6 * 2**20, transcendentals=0),
    )(table, window, voltages, following, early)


def gram_kernel(frame_total, slots, spectra, tiles, wide, lefts, rights, row_scale, col_scale, grid_tiles):
    channel = pl.program_id(0)
    blocks = grid_tiles.shape[0]
    width = grid_tiles.shape[2]
    times = spectra.shape[0] // blocks
    pieces = spectra.shape[2] // LANES
    parts = spectra.shape[1]
    depth = times * pieces

    @pl.when(channel == 0)
    def _():
        def unpack(n, carry):
            t, b = n // blocks, n % blocks
            rows = spectra[n].astype(jnp.float32)
            for p in range(pieces):
                at = pl.multiple_of((t * pieces + p) * parts, parts)
                wide[b, pl.ds(at, parts), :] = rows[:, p * LANES : (p + 1) * LANES]
            return carry

        lax.fori_loop(0, times * blocks, unpack, 0)

    low = lax.broadcasted_iota(jnp.int32, (depth, LANES), 1) < width
    half = LANES // 2
    turn = lambda x: pltpu.roll(x, half, 1)

    def matrix(b):
        re = wide[b, pl.ds(channel * 2, depth, stride=parts), :]
        im = wide[b, pl.ds(channel * 2 + 1, depth, stride=parts), :]
        return (jnp.where(low, re, turn(im)), jnp.where(low, turn(re), im))

    def scale(power):
        return 1.0 / jnp.sqrt(power / frame_total + 1e-6)

    def build(q, carry):
        pair = [matrix(2 * q), matrix(2 * q + 1)]
        for n, halves in enumerate(pair):
            lanes = slice(n * LANES, (n + 1) * LANES)
            power = jnp.zeros((1, LANES), jnp.float32)
            for h, x in enumerate(halves):
                rolled = turn(x)
                rights[q, h * depth : (h + 1) * depth, lanes] = jnp.where(low, x, -x).astype(jnp.bfloat16)
                rights[q, (2 + h) * depth : (3 + h) * depth, lanes] = rolled.astype(jnp.bfloat16)
                power = power + jnp.sum(x * x + rolled * rolled, axis=0, keepdims=True)
            col_scale[q, :, lanes] = scale(power)
        for h in range(2):
            x, y = pair[0][h], pair[1][h]
            re = jnp.where(low, x, turn(y))
            im = jnp.where(low, turn(x), y)
            if h == 0:
                first = (re, im)
        flat = jnp.concatenate([first[0], re, first[1], im], axis=0).T
        rows = pl.ds(pl.multiple_of(q * LANES, LANES), LANES)
        lefts[rows, :] = flat.astype(jnp.bfloat16)
        row_scale[rows, :] = scale(jnp.sum(flat * flat, axis=1, keepdims=True)) / frame_total
        return carry

    lax.fori_loop(0, blocks // 2, build, 0)

    for q in range(blocks // 2):
        rows = (q + 1) * LANES
        product = jnp.dot(lefts[:rows, :], rights[q], preferred_element_type=jnp.float32)
        product = (product * row_scale[:rows, :] * col_scale[q]).astype(jnp.bfloat16)
        for a in range(2 * q + 2):
            for n in range(2):
                grid_tiles[a, 2 * q + n] = product[a * width : (a + 1) * width, n * LANES : (n + 1) * LANES]

    per_owner = tiles.shape[2]

    def pick(s, carry):
        a, b = slots[s, 0], slots[s, 1]
        tile = grid_tiles[jnp.maximum(a, 0), jnp.maximum(b, 0)]
        tiles[s // per_owner, 0, s % per_owner] = jnp.where(a >= 0, tile, jnp.zeros_like(tile))
        return carry

    lax.fori_loop(0, slots.shape[0], pick, 0, unroll=4)


def all_tiles(spectra, tile_table, blocks, width, frame_total):
    parts = spectra.shape[1]
    channels = parts // 2
    times = spectra.shape[0] // blocks
    depth = times * spectra.shape[2] // LANES
    owners = blocks
    per_owner = tile_table.shape[0] // owners

    def body(*refs):
        gram_kernel(float(frame_total), *refs)

    return pl.pallas_call(
        body,
        name="gram",
        grid_spec=pltpu.PrefetchScalarGridSpec(
            num_scalar_prefetch=1,
            grid=(channels,),
            in_specs=[pl.BlockSpec(spectra.shape, lambda c, s: (0, 0, 0))],
            out_specs=pl.BlockSpec((owners, 1, per_owner, width, 2 * width), lambda c, s: (0, c, 0, 0, 0)),
            scratch_shapes=[
                pltpu.VMEM((blocks, depth * parts, LANES), jnp.float32),
                pltpu.VMEM((blocks * width, 4 * depth), jnp.bfloat16),
                pltpu.VMEM((blocks // 2, 4 * depth, 2 * LANES), jnp.bfloat16),
                pltpu.VMEM((blocks * width, 1), jnp.float32),
                pltpu.VMEM((blocks // 2, 1, 2 * LANES), jnp.float32),
                pltpu.VMEM((blocks, blocks, width, 2 * width), jnp.bfloat16),
            ],
        ),
        out_shape=jax.ShapeDtypeStruct((owners, channels, per_owner, width, 2 * width), jnp.bfloat16),
        cost_estimate=pl.CostEstimate(flops=3 * 10**9, bytes_accessed=12 * 2**20, transcendentals=0),
    )(tile_table, spectra)


def on_device(voltages, tile_table):
    width, local_len = voltages.shape
    blocks = lax.axis_size("inp")
    devices = blocks * lax.axis_size("chan")
    frame_total = local_len // L * lax.axis_size("chan")
    spectra = channelize(voltages)
    spectra = spectra.reshape(devices, 2 * NCH // devices, spectra.shape[1])
    turned = lax.all_to_all(spectra, EVERY, 0, 0, tiled=True)
    tiles = all_tiles(turned, tile_table, blocks, width, frame_total)
    tiles = lax.all_to_all(tiles, "inp", 0, 0, tiled=True)
    return tiles.astype(jnp.float32).reshape(-1, *tiles.shape[2:])


def solution(mesh):
    return jax.shard_map(
        on_device,
        mesh=mesh,
        in_specs=(P("inp", "chan"), P()),
        out_specs=P("chan", "inp", None, None),
        check_vma=False,
    )
```

time: 445 us -> 219 us (0.49)
  waiting for transfers between devices: 198 us -> 29 us
  blocking collectives: 37.1 us -> 111 us
  local copies, waits for them, and re-layouts: 66.6 us -> 4.16 us
  other arithmetic: 62.7 us -> 13 us
  Pallas kernels: 0 us -> 48.1 us
  matrix products: 46.3 us -> 0 us
  loops' own time: 17.5 us -> 0 us
  between operations: 13.6 us -> 0.05 us
  starting transfers between devices: 1.47 us -> 13.2 us
    all_gather x1 -> x0, waiting for transfers between devices: 198 us -> none  [on_device(): everything = lax.all_gather(own, 'inp', axis=1, tiled=True)]
    all_to_all x2 -> x1, blocking collectives: 37.1 us -> 111 us  [on_device(): tiles = lax.all_to_all(tiles, 'inp', 0, 0, tiled=True)]
    pallas_call x0 -> x3, Pallas kernels: none -> 48.1 us  [the longest x1 28.5 us: all_tiles(): pl.pallas_call(body, name='gram', grid_spec=pltpu.PrefetchScalarGridSpec(...]
    dot_general x10 -> x0, matrix products: 46.3 us -> none  [the longest x9 41.6 us: make_tile(): jnp.einsum('cif,cjf->cij', left_rows, partner, preferred_element_type=jnp...]
    all_to_all x0 -> x1, waiting for transfers between devices: none -> 29 us  [on_device(): turned = lax.all_to_all(spectra, EVERY, 0, 0, tiled=True)]
    dynamic_slice x28 -> x0, local copies, waits for them, and re-layouts: 22.1 us -> none  [the longest x9 15.7 us: make_tile(): lax.dynamic_slice_in_dim(everything, second * block_width, block_width, 1)]
    another operation x2 -> x0, other arithmetic: 19.4 us -> none
    neg x9 -> x0, other arithmetic: 18.8 us -> none  [rotate_parts(): -rows[..., half_width:]]
  transfers between devices with their start and end apart: 2 -> 2, of which waited for: 1 -> 1; matrix products, arithmetic and copies ran while one was open for 9% -> 0% of each run, Pallas kernels for 0% -> 6%
where the time goes in v1:
time: 219 us
  blocking collectives  111 us (51%)
  Pallas kernels  48.1 us (22%)
  waiting for transfers between devices  29 us (13%)
  starting transfers between devices  13.2 us (6%)
  other arithmetic  13 us (6%)
  local copies, waits for them, and re-layouts  4.16 us (2%)
    all_to_all x1, blocking collectives, on_device(): tiles = lax.all_to_all(tiles, 'inp', 0, 0, tiled=True)  111 us
    all_to_all x1, waiting for transfers between devices, on_device(): turned = lax.all_to_all(spectra, EVERY, 0, 0, tiled=True)  29 us
    pallas_call x1, Pallas kernels, all_tiles(): pl.pallas_call(body, name='gram', grid_spec=pltpu.PrefetchScalarGridSpec(...  28.5 us
    pallas_call x1, Pallas kernels, channelize(): pl.pallas_call(early_kernel, name='channelize_early', grid=(steps - 1,),...  13.4 us
    reshape x1, other arithmetic, on_device(): return tiles.astype(jnp.float32).reshape(-1, *tiles.shape[2:])  13 us
    all_to_all x1, starting transfers between devices, on_device(): turned = lax.all_to_all(spectra, EVERY, 0, 0, tiled=True)  11.9 us
    pallas_call x1, Pallas kernels, channelize(): pl.pallas_call(late_kernel, name='channelize_late', grid=(1,), in_specs=[...  6.26 us
  transfers between devices with their start and end apart: 2, of which 1 were waited for; matrix products, arithmetic and copies ran while one was open for 0% of the time, Pallas kernels for 6%

profile of v1, /device:TPU:0, one launch (start us, length us, event | category | flops | bytes accessed | tf_op | source)
XLA Modules:
  0.0 218.8 jit_solution(17971842628224652249)
XLA Ops:
  0.0 1.2 slice.3
  1.2 1.3 collective-permute-start
  2.5 13.4 %channelize_early.1 = (bf16[1024,1024]{1,0:T(8,128)(2,1)}, bf16[1024,2048]{1,0:T(8,128)(2,1)}) custom-call(f32[32,2048]{1,0:T(8,128)} %constant.11.clone.cc, f32[32,2048]{1,0:T(8,128)} %constant.12.clone.cs, f32[32,2048]{1,0:T(8,128)} %constant.13.clone.fc, f32[32,2048]{1,0:T(8,128)} %constant.14.clone.fs, f32[4,2048]{1,0:T(4,128)} %constant.10.clone.window, ...), custom_call_target="tpu_custom_call" | custom-call | flops 3000000000 | bytes 12582912 | tf_op jit(solution)/shard_map/channelize_early/pallas_call | solution.py:117
  15.9 0.0 copy-start.2
  15.9 0.0 collective-permute-done.following
  15.9 0.0 copy-start.1
  15.9 0.9 copy-done.1
  16.8 6.3 %channelize_late.1 = bf16[1024,1024]{1,0:T(8,128)(2,1)} custom-call(bf16[1024,2048]{1,0:T(8,128)(2,1)} %get-tuple-element.7.table, f32[4,2048]{1,0:T(4,128)} %constant.10.clone.window, bf16[64,32768]{1,0:T(8,128)(2,1)} %current.3, bf16[64,6144]{1,0:T(8,128)(2,1)} %copy-done.1, ...), custom_call_target="tpu_custom_call", output_to_operand_aliasing={{}: (4, {})} | custom-call | flops 1000000000 | bytes 6291456 | tf_op jit(solution)/shard_map/channelize_late/pallas_call | solution.py:132
  23.1 11.9 %all-to-all-start = ((bf16[128,8,1024]{2,1,0:T(8,128)(2,1)}), bf16[128,8,1024]{2,1,0:T(8,128)(2,1)S(1)}, u32[]{:S(2)}, u32[]{:S(2)}) async-start(bf16[128,8,1024]{2,1,0:T(8,128)(2,1)} %bitcast.4), calls=%async_computation | async-start | bytes 4194304 | tf_op jit(solution)/shard_map/all_to_all | solution.py:268
  35.0 0.0 copy-done.2
  35.0 0.7 copy.9.refs_0_
  35.7 29.0 %all-to-all-done.refs_1_ = bf16[128,8,1024]{2,1,0:T(8,128)(2,1)S(1)} async-done(((bf16[128,8,1024]{2,1,0:T(8,128)(2,1)}), bf16[128,8,1024]{2,1,0:T(8,128)(2,1)S(1)}, u32[]{:S(2)}, u32[]{:S(2)}) %all-to-all-start) | async-done | bytes 2097184 | tf_op jit(solution)/shard_map/all_to_all | solution.py:268
  64.8 0.0 copy-start
  64.8 1.4 copy-done
  66.1 28.5 %gram.1 = bf16[16,4,9,64,128]{4,3,2,1,0:T(8,128)(2,1)} custom-call(s32[144,2]{1,0:T(8,128)} %copy.9.refs_0_, bf16[128,8,1024]{2,1,0:T(8,128)(2,1)} %copy-done), custom_call_target="tpu_custom_call" | custom-call | flops 3000000000 | bytes 12582912 | tf_op jit(solution)/shard_map/gram/pallas_call | solution.py:239
  94.6 111.3 %all_to_all.10 = bf16[16,4,9,64,128]{4,3,2,1,0:T(8,128)(2,1)} all-to-all(bf16[16,4,9,64,128]{4,3,2,1,0:T(8,128)(2,1)} %gram.1), channel_id=1, replica_groups=mesh['chan'=8,'inp'=16] {'inp'}, dimensions={0} | all-to-all | bytes 18874368 | tf_op jit(solution)/shard_map/all_to_all | solution.py:270
  205.8 13.0 %bitcast_convert_fusion = f32[64,9,64,128]{3,2,1,0:T(8,128)} fusion(bf16[16,4,9,64,128]{4,3,2,1,0:T(8,128)(2,1)} %all_to_all.10), kind=kLoop, calls=%fused_computation | loop fusion | flops 4718592 | bytes 28311552 | tf_op jit(solution)/shard_map/reshape | solution.py:271
Async XLA Ops:
  1.2 14.7 %collective-permute-start = (bf16[64,6144]{1,0:T(8,128)(2,1)S(1)}, bf16[64,6144]{1,0:T(8,128)(2,1)S(1)}, u32[]{:S(2)}, u32[]{:S(2)}) collective-permute-start(bf16[64,6144]{1,0:T(8,128)(2,1)S(1)} %slice.3), channel_id=1, source_target_pairs={{16,0},{32,16},{48,32},{64,48},{80,64},{96,80},{112,96},{17,1},{33... | collective-permute-start | bytes 2359304 | tf_op jit(solution)/shard_map/ppermute | solution.py:111
  15.9 19.1 %copy-start.2 = (s32[144,2]{0,1:T(2,128)S(1)}, s32[144,2]{0,1:T(2,128)}, u32[]{:S(2)}) copy-start(s32[144,2]{0,1:T(2,128)} %param.8) | copy-start | bytes 3460
  15.9 0.9 copy-start.1
  23.1 41.7 %all-to-all-start = ((bf16[128,8,1024]{2,1,0:T(8,128)(2,1)}), bf16[128,8,1024]{2,1,0:T(8,128)(2,1)S(1)}, u32[]{:S(2)}, u32[]{:S(2)}) async-start(bf16[128,8,1024]{2,1,0:T(8,128)(2,1)} %bitcast.4), calls=%async_computation | async-start | bytes 4194304 | tf_op jit(solution)/shard_map/all_to_all | solution.py:268
  64.8 1.4 copy-start

commit v2 on v1

v2 whole, which is shorter than its diff:
```python
import functools
import math

import jax
import jax.numpy as jnp
import numpy as np
from jax import lax
from jax.experimental import pallas as pl
from jax.experimental.pallas import tpu as pltpu
from jax.sharding import PartitionSpec as P

L = 2048
NCH = 512
TAPS = 4
LANES = 128
STEP = 4
COARSE = 16
EVERY = ("chan", "inp")


def filter_window():
    positions = np.arange(TAPS * L, dtype=np.float64)
    tapering = 0.5 - 0.5 * np.cos(2.0 * math.pi * positions / (TAPS * L))
    shape_sinc = np.sinc((positions - TAPS * L / 2.0) / L)
    return (shape_sinc * tapering).reshape(TAPS, L).astype(np.float32)


def twiddle_factors():
    samples = np.arange(L)[None, :]
    coarse = (COARSE * np.arange(NCH // COARSE)[:, None] * samples) % L
    rows = np.arange(2 * COARSE)[:, None]
    fine = ((rows // 2) * samples + (rows % 2) * (L // 4)) % L
    unit = 2.0 * math.pi / L
    tables = [np.cos(coarse * unit), np.sin(coarse * unit), np.cos(fine * unit), np.sin(fine * unit)]
    return [t.astype(np.float32) for t in tables]


def build_table(coarse_cos, coarse_sin, fine_cos, fine_sin, table):
    rows = 2 * COARSE

    def column(j, carry):
        lanes = pl.ds(pl.multiple_of(j * LANES, LANES), LANES)
        fc = fine_cos[:, lanes]
        fs = fine_sin[:, lanes]
        for a in range(NCH // COARSE):
            part = coarse_cos[a : a + 1, lanes] * fc - coarse_sin[a : a + 1, lanes] * fs
            table[a * rows : (a + 1) * rows, lanes] = part.astype(jnp.bfloat16)
        return carry

    lax.fori_loop(0, L // LANES, column, 0)


def filter_frames(window, current, following, filtered):
    width = current.shape[0]

    def column(j, carry):
        taps = [window[k : k + 1, pl.ds(pl.multiple_of(j * LANES, LANES), LANES)] for k in range(TAPS)]
        for r in range(0, width, 16):
            rows = slice(r, r + 16)
            frames = []
            for f in range(STEP + TAPS - 1):
                source, at = (current, f) if f < STEP else (following, f - STEP)
                lanes = pl.ds(pl.multiple_of(j * LANES + at * L, LANES), LANES)
                frames.append(source[rows, lanes].astype(jnp.float32))
            for f in range(STEP):
                total = frames[f] * taps[0]
                for k in range(1, TAPS):
                    total = total + frames[f + k] * taps[k]
                filtered[f * width + r : f * width + r + 16, pl.ds(pl.multiple_of(j * LANES, LANES), LANES)] = (
                    total.astype(jnp.bfloat16)
                )
        return carry

    lax.fori_loop(0, L // LANES, column, 0)


def transform(table, filtered, spectra):
    rows = 512

    def chunk(i, carry):
        at = pl.ds(pl.multiple_of(i * rows, rows), rows)
        product = lax.dot_general(
            table[at, :], filtered[...], (((1,), (1,)), ((), ())), preferred_element_type=jnp.float32
        )
        spectra[at, :] = product.astype(jnp.bfloat16)
        return carry

    lax.fori_loop(0, 2 * NCH // rows, chunk, 0)


def channelize_kernel(cc, cs, fc, fs, window, current, following, *refs):
    spectra, table, filtered = refs[-3:]

    @pl.when(pl.program_id(0) == 0)
    def _():
        build_table(cc, cs, fc, fs, table)

    filter_frames(window, current, following, filtered)
    transform(table, filtered, spectra)


def channelize(voltages):
    width, local_len = voltages.shape
    steps = local_len // (STEP * L)
    span = STEP * L
    halo = (TAPS - 1) * L
    devices = lax.axis_size("chan")
    halo_frames = lax.ppermute(voltages[:, :halo], "chan", [(i, i - 1) for i in range(1, devices)])
    window = jnp.asarray(filter_window())
    factors = [jnp.asarray(t) for t in twiddle_factors()]
    columns = STEP * width
    whole = lambda shape: pl.BlockSpec(shape, lambda *_: (0, 0), pipeline_mode=pl.Buffered(1))

    def call(name, first, count, following, earlier):
        given = [] if earlier is None else [earlier]
        if following is voltages:
            following_spec = pl.BlockSpec((width, span), lambda j: (0, first + j + 1))
        else:
            following_spec = whole((width, halo))
        return pl.pallas_call(
            channelize_kernel,
            name=name,
            grid=(count,),
            in_specs=[whole(t.shape) for t in factors]
            + [
                whole((TAPS, L)),
                pl.BlockSpec((width, span), lambda j: (0, first + j)),
                following_spec,
            ]
            + [pl.BlockSpec(memory_space=pl.ANY)] * len(given),
            out_specs=pl.BlockSpec((2 * NCH, columns), lambda j: (0, first + j)),
            out_shape=jax.ShapeDtypeStruct((2 * NCH, steps * columns), jnp.bfloat16),
            scratch_shapes=[pltpu.VMEM((2 * NCH, L), jnp.bfloat16), pltpu.VMEM((columns, L), jnp.bfloat16)],
            input_output_aliases={7: 0} if given else {},
            cost_estimate=pl.CostEstimate(flops=count * 10**9, bytes_accessed=6 * 2**20, transcendentals=0),
        )(*factors, window, voltages, following, *given)

    early = call("channelize_early", 0, steps - 1, voltages, None)
    return call("channelize_late", steps - 1, 1, halo_frames, early)


def gram_kernel(frame_total, slots, spectra, tiles, wide, lefts, rights, row_scale, col_scale, places):
    channel = pl.program_id(0)
    width = tiles.shape[1]
    blocks = lefts.shape[0] // width
    owners = blocks
    channels = spectra.shape[1] // 2
    per_owner = tiles.shape[0] // (owners * channels)
    times = spectra.shape[0] // blocks
    pieces = spectra.shape[2] // LANES
    parts = spectra.shape[1]
    depth = times * pieces

    @pl.when(channel == 0)
    def _():
        def unpack(b, carry):
            for t in range(times):
                rows = spectra[t * blocks + b].astype(jnp.float32)
                for p in range(pieces):
                    at = (t * pieces + p) * parts
                    wide[b, at : at + parts, :] = rows[:, p * LANES : (p + 1) * LANES]
            return carry

        lax.fori_loop(0, blocks, unpack, 0)

        def note(owner, carry):
            for k in range(per_owner):
                a, b = slots[owner * per_owner + k, 0], slots[owner * per_owner + k, 1]
                place = owner * (channels * per_owner) + k

                @pl.when(a >= 0)
                def _():
                    places[a * blocks + b] = place

                @pl.when(a < 0)
                def _():
                    for c in range(channels):
                        tiles[place + c * per_owner] = jnp.zeros((width, LANES), jnp.bfloat16)

            return carry

        lax.fori_loop(0, owners, note, 0)

    low = lax.broadcasted_iota(jnp.int32, (depth, LANES), 1) < width
    turn = lambda x: pltpu.roll(x, LANES // 2, 1)

    def scale(power):
        return lax.rsqrt(power / frame_total + 1e-6)

    def build(q, carry):
        pair = []
        for n in range(2):
            re = wide[2 * q + n, pl.ds(2 * channel, depth, stride=parts), :]
            im = wide[2 * q + n, pl.ds(2 * channel + 1, depth, stride=parts), :]
            re_turned, im_turned = turn(re), turn(im)
            pair.append((re, re_turned, im, im_turned))
            lanes = slice(n * LANES, (n + 1) * LANES)
            right = (
                jnp.where(low, re, -im_turned),
                jnp.where(low, re_turned, -im),
                jnp.where(low, im, re_turned),
                jnp.where(low, im_turned, re),
            )
            for k, part in enumerate(right):
                rights[q, k * depth : (k + 1) * depth, lanes] = part.astype(jnp.bfloat16)
            power = jnp.sum(re * re + im * im, axis=0, keepdims=True)
            col_scale[q, :, lanes] = scale(power + turn(power))
        x, y = pair
        flat = [jnp.where(low, x[k], y[k ^ 1]) for k in range(4)]
        flat = jnp.concatenate(flat, axis=0).astype(jnp.bfloat16).T
        rows = pl.ds(pl.multiple_of(q * LANES, LANES), LANES)
        lefts[rows, :] = flat
        flat = flat.astype(jnp.float32)
        row_scale[rows, :] = scale(jnp.sum(flat * flat, axis=1, keepdims=True)) / frame_total
        return carry

    lax.fori_loop(0, blocks // 2, build, 0)

    offset = channel * per_owner
    for q in range(blocks // 2):
        rows = (q + 1) * LANES
        product = jnp.dot(lefts[:rows, :], rights[q], preferred_element_type=jnp.float32)
        product = (product * row_scale[:rows, :] * col_scale[q]).astype(jnp.bfloat16)
        for n in range(2):
            for a in range(2 * q + n + 1):
                tile = product[a * width : (a + 1) * width, n * LANES : (n + 1) * LANES]
                tiles[places[a * blocks + 2 * q + n] + offset] = tile


def all_tiles(spectra, tile_table, blocks, width, frame_total):
    parts = spectra.shape[1]
    channels = parts // 2
    times = spectra.shape[0] // blocks
    depth = times * spectra.shape[2] // LANES
    per_owner = tile_table.shape[0] // blocks
    return pl.pallas_call(
        functools.partial(gram_kernel, float(frame_total)),
        name="gram",
        grid_spec=pltpu.PrefetchScalarGridSpec(
            num_scalar_prefetch=1,
            grid=(channels,),
            in_specs=[pl.BlockSpec(spectra.shape, lambda c, s: (0, 0, 0), pipeline_mode=pl.Buffered(1))],
            out_specs=pl.BlockSpec(memory_space=pltpu.VMEM),
            scratch_shapes=[
                pltpu.VMEM((blocks, depth * parts, LANES), jnp.float32),
                pltpu.VMEM((blocks * width, 4 * depth), jnp.bfloat16),
                pltpu.VMEM((blocks // 2, 4 * depth, 2 * LANES), jnp.bfloat16),
                pltpu.VMEM((blocks * width, 1), jnp.float32),
                pltpu.VMEM((blocks // 2, 1, 2 * LANES), jnp.float32),
                pltpu.SMEM((blocks * blocks,), jnp.int32),
            ],
        ),
        out_shape=jax.ShapeDtypeStruct((blocks * channels * per_owner, width, 2 * width), jnp.bfloat16),
        compiler_params=pltpu.CompilerParams(vmem_limit_bytes=32 * 2**20),
        cost_estimate=pl.CostEstimate(flops=3 * 10**9, bytes_accessed=12 * 2**20, transcendentals=0),
    )(tile_table, spectra)


def widen_kernel(tiles, out):
    out[...] = tiles[...].astype(jnp.float32)


def widen(tiles):
    sources, channels, per_owner, width, lanes = tiles.shape
    block = (1, channels, per_owner, width, lanes)
    at = lambda d: (d, 0, 0, 0, 0)
    return pl.pallas_call(
        widen_kernel,
        name="widen",
        grid=(sources,),
        in_specs=[pl.BlockSpec(block, at)],
        out_specs=pl.BlockSpec(block, at),
        out_shape=jax.ShapeDtypeStruct(tiles.shape, jnp.float32),
        compiler_params=pltpu.CompilerParams(vmem_limit_bytes=24 * 2**20),
        cost_estimate=pl.CostEstimate(flops=0, bytes_accessed=28 * 2**20, transcendentals=0),
    )(tiles)


def on_device(voltages, tile_table):
    width, local_len = voltages.shape
    blocks = lax.axis_size("inp")
    devices = blocks * lax.axis_size("chan")
    frame_total = local_len // L * lax.axis_size("chan")
    spectra = channelize(voltages)
    spectra = spectra.reshape(devices, 2 * NCH // devices, spectra.shape[1])
    turned = lax.all_to_all(spectra, EVERY, 0, 0, tiled=True)
    tiles = all_tiles(turned, tile_table, blocks, width, frame_total)
    tiles = tiles.reshape(blocks, -1, tile_table.shape[0] // blocks, *tiles.shape[1:])
    out = widen(lax.all_to_all(tiles, "inp", 0, 0, tiled=True))
    return out.reshape(-1, *out.shape[2:])


def solution(mesh):
    return jax.shard_map(
        on_device,
        mesh=mesh,
        in_specs=(P("inp", "chan"), P()),
        out_specs=P("chan", "inp", None, None),
        check_vma=False,
    )
```

time: 219 us -> 197 us (0.90)
  other arithmetic: 13 us -> 0 us
  Pallas kernels: 48.1 us -> 41.4 us
    reshape x1 -> x0, other arithmetic: 13 us -> none  [on_device(): return tiles.astype(jnp.float32).reshape(-1, *tiles.shape[2:])]
    pallas_call x3 -> x4, Pallas kernels: 48.1 us -> 41.4 us  [the longest x2 16.9 us: call(): pl.pallas_call(channelize_kernel, name=name, grid=(count,), in_specs=[who...]
where the time goes in v2:
time: 197 us
  blocking collectives  110 us (56%)
  Pallas kernels  41.4 us (21%)
  waiting for transfers between devices  29.7 us (15%)
  starting transfers between devices  13.2 us (7%)
  local copies, waits for them, and re-layouts  2.18 us (1%)
    all_to_all x1, blocking collectives, on_device(): out = widen(lax.all_to_all(tiles, 'inp', 0, 0, tiled=True))  110 us
    all_to_all x1, waiting for transfers between devices, on_device(): turned = lax.all_to_all(spectra, EVERY, 0, 0, tiled=True)  29.7 us
    pallas_call x2, Pallas kernels, call(): pl.pallas_call(channelize_kernel, name=name, grid=(count,), in_specs=[who...  16.9 us
    pallas_call x1, Pallas kernels, all_tiles(): pl.pallas_call(functools.partial(gram_kernel, float(frame_total)), name='...  15.4 us
    all_to_all x1, starting transfers between devices, on_device(): turned = lax.all_to_all(spectra, EVERY, 0, 0, tiled=True)  11.9 us
    pallas_call x1, Pallas kernels, widen(): pl.pallas_call(widen_kernel, name='widen', grid=(sources,), in_specs=[pl....  9.1 us
  transfers between devices with their start and end apart: 2, of which 1 were waited for; matrix products, arithmetic and copies ran while one was open for 0% of the time, Pallas kernels for 6%

profile of v2, /device:TPU:0, one launch (start us, length us, event | category | flops | bytes accessed | tf_op | source)
XLA Modules:
  0.0 196.7 jit_solution(12831029737425251018)
XLA Ops:
  0.0 1.2 slice.3
  1.2 1.3 collective-permute-start
  2.5 10.8 %channelize_early.1.refs_0_ = bf16[1024,1024]{1,0:T(8,128)(2,1)} custom-call(f32[32,2048]{1,0:T(8,128)} %constant.11.clone.cc, f32[32,2048]{1,0:T(8,128)} %constant.12.clone.cs, f32[32,2048]{1,0:T(8,128)} %constant.13.clone.fc, f32[32,2048]{1,0:T(8,128)} %constant.14.clone.fs, f32[4,2048]{1,0:T(4,128)} %constant.10.clone.window, bf16[64,32768]{1,0:T(8,128)(2,1)} %current.3, ...), custom_call_target="tpu_custom_call" | custom-call | flops 3000000000 | bytes 6291456 | tf_op jit(solution)/shard_map/channelize_early/pallas_call | solution.py:120
  13.3 0.0 collective-permute-done.following
  13.3 0.0 copy-start
  13.3 0.9 copy-done
  14.2 6.1 %channelize_late.1 = bf16[1024,1024]{1,0:T(8,128)(2,1)} custom-call(f32[32,2048]{1,0:T(8,128)} %constant.11.clone.cc, f32[32,2048]{1,0:T(8,128)} %constant.12.clone.cs, f32[32,2048]{1,0:T(8,128)} %constant.13.clone.fc, f32[32,2048]{1,0:T(8,128)} %constant.14.clone.fs, f32[4,2048]{1,0:T(4,128)} %constant.10.clone.window, ...), custom_call_target="tpu_custom_call", output_to_operand_aliasing={{}: (7, {})} | custom-call | flops 1000000000 | bytes 6291456 | tf_op jit(solution)/shard_map/channelize_late/pallas_call | solution.py:120
  20.3 0.0 copy-start.1
  20.3 11.9 %all-to-all-start = ((bf16[128,8,1024]{2,1,0:T(8,128)(2,1)}), bf16[128,8,1024]{2,1,0:T(8,128)(2,1)S(1)}, u32[]{:S(2)}, u32[]{:S(2)}) async-start(bf16[128,8,1024]{2,1,0:T(8,128)(2,1)} %bitcast.4), calls=%async_computation | async-start | bytes 4194304 | tf_op jit(solution)/shard_map/all_to_all | solution.py:286
  32.2 0.0 copy-done.1
  32.2 0.1 copy.9.slots
  32.3 29.7 %all-to-all-done.spectra = bf16[128,8,1024]{2,1,0:T(8,128)(2,1)S(1)} async-done(((bf16[128,8,1024]{2,1,0:T(8,128)(2,1)}), bf16[128,8,1024]{2,1,0:T(8,128)(2,1)S(1)}, u32[]{:S(2)}, u32[]{:S(2)}) %all-to-all-start) | async-done | bytes 2097184 | tf_op jit(solution)/shard_map/all_to_all | solution.py:286
  62.0 15.4 %gram.1 = bf16[576,64,128]{2,1,0:T(8,128)(2,1)S(1)} custom-call(s32[144,2]{1,0:T(8,128)S(1)} %copy.9.slots, bf16[128,8,1024]{2,1,0:T(8,128)(2,1)S(1)} %all-to-all-done.spectra), custom_call_target="tpu_custom_call" | custom-call | flops 3000000000 | bytes 12582912 | tf_op jit(solution)/shard_map/gram/pallas_call | solution.py:236
  77.4 110.3 %all_to_all.10.tiles = bf16[16,4,9,64,128]{4,3,2,1,0:T(8,128)(2,1)S(1)} all-to-all(bf16[16,4,9,64,128]{4,3,2,1,0:T(8,128)(2,1)S(1)} %bitcast.3), channel_id=1, replica_groups=mesh['chan'=8,'inp'=16] {'inp'}, dimensions={0} | all-to-all | bytes 18874368 | tf_op jit(solution)/shard_map/all_to_all | solution.py:289
  187.6 9.1 %widen.1 = f32[16,4,9,64,128]{4,3,2,1,0:T(8,128)} custom-call(bf16[16,4,9,64,128]{4,3,2,1,0:T(8,128)(2,1)S(1)} %all_to_all.10.tiles), custom_call_target="tpu_custom_call" | custom-call | bytes 29360128 | tf_op jit(solution)/shard_map/widen/pallas_call | solution.py:267
Async XLA Ops:
  1.2 12.1 %collective-permute-start = (bf16[64,6144]{1,0:T(8,128)(2,1)S(1)}, bf16[64,6144]{1,0:T(8,128)(2,1)S(1)}, u32[]{:S(2)}, u32[]{:S(2)}) collective-permute-start(bf16[64,6144]{1,0:T(8,128)(2,1)S(1)} %slice.3), channel_id=1, source_target_pairs={{16,0},{32,16},{48,32},{64,48},{80,64},{96,80},{112,96},{17,1},{33... | collective-permute-start | bytes 2359304 | tf_op jit(solution)/shard_map/ppermute | solution.py:108
  13.3 0.9 copy-start
  20.3 11.9 %copy-start.1 = (s32[144,2]{0,1:T(2,128)S(1)}, s32[144,2]{0,1:T(2,128)}, u32[]{:S(2)}) copy-start(s32[144,2]{0,1:T(2,128)} %param.8) | copy-start | bytes 3460
  20.3 41.7 %all-to-all-start = ((bf16[128,8,1024]{2,1,0:T(8,128)(2,1)}), bf16[128,8,1024]{2,1,0:T(8,128)(2,1)S(1)}, u32[]{:S(2)}, u32[]{:S(2)}) async-start(bf16[128,8,1024]{2,1,0:T(8,128)(2,1)} %bitcast.4), calls=%async_computation | async-start | bytes 4194304 | tf_op jit(solution)/shard_map/all_to_all | solution.py:286

commit v3 on v2

v3 whole, which is shorter than its diff:
```python
import functools
import math

import jax
import jax.numpy as jnp
import numpy as np
from jax import lax
from jax.experimental import pallas as pl
from jax.experimental.pallas import tpu as pltpu
from jax.sharding import PartitionSpec as P

L = 2048
NCH = 512
TAPS = 4
LANES = 128
STEP = 4
COARSE = 16
EVERY = ("chan", "inp")


def filter_window():
    positions = np.arange(TAPS * L, dtype=np.float64)
    tapering = 0.5 - 0.5 * np.cos(2.0 * math.pi * positions / (TAPS * L))
    shape_sinc = np.sinc((positions - TAPS * L / 2.0) / L)
    return (shape_sinc * tapering).reshape(TAPS, L).astype(np.float32)


def twiddle_factors():
    unit = 2.0 * math.pi / L
    coarse = (COARSE * np.arange(NCH // COARSE)[:, None] * np.arange(L // COARSE)[None, :]) % L
    rows = np.arange(2 * COARSE)[:, None]
    fine = ((rows // 2) * np.arange(L // 2)[None, :] + (rows % 2) * (L // 4)) % L
    both = lambda phases: np.concatenate([np.cos(phases * unit), np.sin(phases * unit)]).astype(np.float32)
    return both(coarse), both(fine)


def build_table(coarse, fine, table):
    rows = 2 * COARSE
    groups = NCH // COARSE
    channel = lax.broadcasted_iota(jnp.int32, (rows, LANES), 0) // 2
    later = jnp.where(channel % 2 == 0, 1.0, -1.0).astype(jnp.float32)

    def column(j, carry):
        lanes = pl.ds(pl.multiple_of(j * LANES, LANES), LANES)
        lanes_later = pl.ds(pl.multiple_of(j * LANES + L // 2, LANES), LANES)
        fine_cos, fine_sin = fine[:rows, lanes], fine[rows:, lanes]
        for a in range(groups):
            part = coarse[a : a + 1, :] * fine_cos - coarse[groups + a : groups + a + 1, :] * fine_sin
            table[a * rows : (a + 1) * rows, lanes] = part.astype(jnp.bfloat16)
            table[a * rows : (a + 1) * rows, lanes_later] = (part * later).astype(jnp.bfloat16)
        return carry

    lax.fori_loop(0, L // 2 // LANES, column, 0)


def filter_column(window, frames, filtered, j):
    width = frames[0][0].shape[0]
    at = pl.ds(pl.multiple_of(j * LANES, LANES), LANES)
    taps = [window[k : k + 1, at] for k in range(TAPS)]
    for r in range(0, width, 16):
        rows = slice(r, r + 16)
        samples = [
            source[rows, pl.ds(pl.multiple_of(first + j * LANES, LANES), LANES)].astype(jnp.float32)
            for source, first in frames
        ]
        for f in range(STEP):
            total = samples[f] * taps[0]
            for k in range(1, TAPS):
                total = total + samples[f + k] * taps[k]
            filtered[f * width + r : f * width + r + 16, at] = total.astype(jnp.bfloat16)


def filter_frames(window, frames, filtered):
    def column(j, carry):
        filter_column(window, frames, filtered, j)
        return carry

    lax.fori_loop(0, L // LANES, column, 0)


def transform(table, filtered, spectra, beside=None):
    rows = 512
    chunks = 2 * NCH // rows
    share = L // LANES // chunks

    def chunk(i, carry):
        at = pl.ds(pl.multiple_of(i * rows, rows), rows)
        product = lax.dot_general(
            table[at, :], filtered[...], (((1,), (1,)), ((), ())), preferred_element_type=jnp.float32
        )
        spectra[at, :] = product.astype(jnp.bfloat16)
        if beside is not None:
            for j in range(share):
                beside(i * share + j)
        return carry

    lax.fori_loop(0, chunks, chunk, 0)


def early_kernel(
    coarse_hbm, fine_hbm, window_hbm, voltages, spectra, table, last, window, coarse, fine, head, even, odd, parts, sems, out_sems
):
    span = STEP * L
    width = even.shape[0]
    steps = spectra.shape[1] // width
    small = [(coarse_hbm, coarse), (fine_hbm, fine), (window_hbm, window)]
    loads = [pltpu.make_async_copy(source, target, sems.at[n]) for n, (source, target) in enumerate(small)]
    copies = []
    for n in range(steps):
        target = last if n == steps - 1 else head.at[:, n * span : (n + 1) * span]
        source = voltages.at[:, n * span : (n + 1) * span]
        copies.append(pltpu.make_async_copy(source, target, sems.at[len(small) + n]))
    for copy in loads + copies:
        copy.start()
    for copy in loads:
        copy.wait()
    build_table(coarse, fine, table)
    places = [(head, f * L) for f in range((steps - 1) * STEP)] + [(last, f * L) for f in range(STEP)]
    frames = lambda n: places[n * STEP : (n + 1) * STEP + TAPS - 1]
    copies[0].wait()
    copies[1].wait()
    filtered = [even, odd]
    filter_frames(window, frames(0), even)
    outs = []
    for n in range(steps - 1):
        beside = None
        if n < steps - 2:
            copies[n + 2].wait()
            beside = lambda j, n=n: filter_column(window, frames(n + 1), filtered[(n + 1) % 2], j)
        transform(table, filtered[n % 2], parts.at[n], beside)
        columns = spectra.at[:, n * width : (n + 1) * width]
        outs.append(pltpu.make_async_copy(parts.at[n], columns, out_sems.at[n]))
        outs[n].start()
    for copy in outs:
        copy.wait()


def late_kernel(table, window, last, following, earlier, spectra, filtered):
    del earlier
    frames = [(last, f * L) for f in range(STEP)] + [(following, f * L) for f in range(TAPS - 1)]
    filter_frames(window, frames, filtered)
    transform(table, filtered, spectra)


def in_hbm(array):
    return pltpu.with_memory_space_constraint(array, pltpu.HBM)


def channelize(voltages):
    width, local_len = voltages.shape
    steps = local_len // (STEP * L)
    span = STEP * L
    halo = (TAPS - 1) * L
    devices = lax.axis_size("chan")
    following = lax.ppermute(voltages[:, :halo], "chan", [(i, i - 1) for i in range(1, devices)])
    constants = [*twiddle_factors(), filter_window()]
    columns = STEP * width
    here = pl.BlockSpec(memory_space=pltpu.VMEM)
    hbm = pl.BlockSpec(memory_space=pltpu.HBM)
    spectra_shape = jax.ShapeDtypeStruct((2 * NCH, steps * columns), jnp.bfloat16)
    filtered = pltpu.VMEM((columns, L), jnp.bfloat16)
    early, table, last, window = pl.pallas_call(
        early_kernel,
        name="channelize_early",
        in_specs=[hbm] * 4,
        out_specs=[hbm, here, here, here],
        out_shape=[
            spectra_shape,
            jax.ShapeDtypeStruct((2 * NCH, L), jnp.bfloat16),
            jax.ShapeDtypeStruct((width, span), jnp.bfloat16),
            jax.ShapeDtypeStruct((TAPS, L), jnp.float32),
        ],
        scratch_shapes=[
            pltpu.VMEM(constants[0].shape, jnp.float32),
            pltpu.VMEM(constants[1].shape, jnp.float32),
            pltpu.VMEM((width, local_len - span), jnp.bfloat16),
            filtered,
            filtered,
            pltpu.VMEM((steps - 1, 2 * NCH, columns), jnp.bfloat16),
            pltpu.SemaphoreType.DMA((3 + steps,)),
            pltpu.SemaphoreType.DMA((steps - 1,)),
        ],
        compiler_params=pltpu.CompilerParams(vmem_limit_bytes=24 * 2**20),
        cost_estimate=pl.CostEstimate(flops=3 * 10**9, bytes_accessed=12 * 2**20, transcendentals=0),
    )(*(in_hbm(jnp.asarray(t)) for t in constants), in_hbm(voltages))
    return pl.pallas_call(
        late_kernel,
        name="channelize_late",
        grid=(1,),
        in_specs=[here] * 4 + [pl.BlockSpec(memory_space=pl.ANY)],
        out_specs=pl.BlockSpec((2 * NCH, columns), lambda j: (0, steps - 1)),
        out_shape=spectra_shape,
        scratch_shapes=[filtered],
        input_output_aliases={4: 0},
        compiler_params=pltpu.CompilerParams(vmem_limit_bytes=24 * 2**20),
        cost_estimate=pl.CostEstimate(flops=10**9, bytes_accessed=6 * 2**20, transcendentals=0),
    )(table, window, last, following, early)


def places_kernel(channels, slots, places):
    blocks = places.shape[1]
    per_owner = slots.shape[0] // blocks

    def owner_slots(owner, empty):
        for k in range(per_owner):
            a, b = slots[owner * per_owner + k, 0], slots[owner * per_owner + k, 1]
            present = a >= 0
            row = jnp.where(present, a, blocks + 1)
            column = jnp.where(present, b, empty)
            places[row, column] = owner * (channels * per_owner) + k
            empty = empty + jnp.where(present, 0, 1)
        return empty

    places[blocks, 0] = lax.fori_loop(0, blocks, owner_slots, 0)


def slot_places(tile_table, blocks, channels):
    return pl.pallas_call(
        functools.partial(places_kernel, channels),
        name="places",
        in_specs=[pl.BlockSpec(memory_space=pltpu.SMEM)],
        out_specs=pl.BlockSpec(memory_space=pltpu.SMEM),
        out_shape=jax.ShapeDtypeStruct((blocks + 2, blocks), jnp.int32),
        cost_estimate=pl.CostEstimate(flops=10**6, bytes_accessed=2**12, transcendentals=0),
    )(tile_table)


def gram_kernel(frame_total, places, spectra, tiles, wide, lefts, rights, row_scale, col_scale):
    channel = pl.program_id(0)
    width = tiles.shape[1]
    blocks = lefts.shape[0] // width
    owners = blocks
    channels = spectra.shape[1] // 2
    per_owner = tiles.shape[0] // (owners * channels)
    times = spectra.shape[0] // blocks
    pieces = spectra.shape[2] // LANES
    parts = spectra.shape[1]
    depth = times * pieces

    @pl.when(channel == 0)
    def _():
        def unpack(b, carry):
            for t in range(times):
                rows = spectra[t * blocks + b].astype(jnp.float32)
                for p in range(pieces):
                    at = (t * pieces + p) * parts
                    wide[b, at : at + parts, :] = rows[:, p * LANES : (p + 1) * LANES]
            return carry

        lax.fori_loop(0, blocks, unpack, 0)

        def clear(n, carry):
            for c in range(channels):
                tiles[places[blocks + 1, n] + c * per_owner] = jnp.zeros((width, LANES), jnp.bfloat16)
            return carry

        lax.fori_loop(0, places[blocks, 0], clear, 0)

    low = lax.broadcasted_iota(jnp.int32, (depth, LANES), 1) < width
    turn = lambda x: pltpu.roll(x, LANES // 2, 1)

    def scale(power):
        return lax.rsqrt(power / frame_total + 1e-6)

    def build(q, carry):
        pair = []
        for n in range(2):
            re = wide[2 * q + n, pl.ds(2 * channel, depth, stride=parts), :]
            im = wide[2 * q + n, pl.ds(2 * channel + 1, depth, stride=parts), :]
            re_turned, im_turned = turn(re), turn(im)
            pair.append((re, re_turned, im, im_turned))
            lanes = slice(n * LANES, (n + 1) * LANES)
            right = (
                jnp.where(low, re, -im_turned),
                jnp.where(low, re_turned, -im),
                jnp.where(low, im, re_turned),
                jnp.where(low, im_turned, re),
            )
            for k, part in enumerate(right):
                rights[q, k * depth : (k + 1) * depth, lanes] = part.astype(jnp.bfloat16)
            power = jnp.sum(re * re + im * im, axis=0, keepdims=True)
            col_scale[q, :, lanes] = scale(power + turn(power))
        x, y = pair
        flat = [jnp.where(low, x[k], y[k ^ 1]) for k in range(4)]
        flat = jnp.concatenate(flat, axis=0).astype(jnp.bfloat16).T
        rows = pl.ds(pl.multiple_of(q * LANES, LANES), LANES)
        lefts[rows, :] = flat
        flat = flat.astype(jnp.float32)
        row_scale[rows, :] = scale(jnp.sum(flat * flat, axis=1, keepdims=True)) / frame_total
        return carry

    lax.fori_loop(0, blocks // 2, build, 0, unroll=2)

    offset = channel * per_owner
    for q in range(blocks // 2):
        rows = (q + 1) * LANES
        product = jnp.dot(lefts[:rows, :], rights[q], preferred_element_type=jnp.float32)
        product = (product * row_scale[:rows, :] * col_scale[q]).astype(jnp.bfloat16)
        for n in range(2):
            for a in range(2 * q + n + 1):
                tile = product[a * width : (a + 1) * width, n * LANES : (n + 1) * LANES]
                tiles[places[a, 2 * q + n] + offset] = tile


def all_tiles(spectra, tile_table, blocks, width, frame_total):
    parts = spectra.shape[1]
    channels = parts // 2
    times = spectra.shape[0] // blocks
    depth = times * spectra.shape[2] // LANES
    per_owner = tile_table.shape[0] // blocks
    return pl.pallas_call(
        functools.partial(gram_kernel, float(frame_total)),
        name="gram",
        grid_spec=pltpu.PrefetchScalarGridSpec(
            num_scalar_prefetch=1,
            grid=(channels,),
            in_specs=[pl.BlockSpec(spectra.shape, lambda c, s: (0, 0, 0), pipeline_mode=pl.Buffered(1))],
            out_specs=pl.BlockSpec(memory_space=pltpu.VMEM),
            scratch_shapes=[
                pltpu.VMEM((blocks, depth * parts, LANES), jnp.float32),
                pltpu.VMEM((blocks * width, 4 * depth), jnp.bfloat16),
                pltpu.VMEM((blocks // 2, 4 * depth, 2 * LANES), jnp.bfloat16),
                pltpu.VMEM((blocks * width, 1), jnp.float32),
                pltpu.VMEM((blocks // 2, 1, 2 * LANES), jnp.float32),
            ],
        ),
        out_shape=jax.ShapeDtypeStruct((blocks * channels * per_owner, width, 2 * width), jnp.bfloat16),
        compiler_params=pltpu.CompilerParams(vmem_limit_bytes=32 * 2**20),
        cost_estimate=pl.CostEstimate(flops=3 * 10**9, bytes_accessed=12 * 2**20, transcendentals=0),
    )(in_hbm(slot_places(tile_table, blocks, channels)), spectra)


def widen_kernel(tiles, out):
    out[...] = tiles[...].astype(jnp.float32)


def widen(tiles):
    sources, channels, per_owner, width, lanes = tiles.shape
    block = (sources // 8, channels, per_owner, width, lanes)
    at = lambda d: (d, 0, 0, 0, 0)
    return pl.pallas_call(
        widen_kernel,
        name="widen",
        grid=(8,),
        in_specs=[pl.BlockSpec(block, at)],
        out_specs=pl.BlockSpec(block, at),
        out_shape=jax.ShapeDtypeStruct(tiles.shape, jnp.float32),
        compiler_params=pltpu.CompilerParams(vmem_limit_bytes=24 * 2**20),
        cost_estimate=pl.CostEstimate(flops=0, bytes_accessed=28 * 2**20, transcendentals=0),
    )(tiles)


def on_device(voltages, tile_table):
    width, local_len = voltages.shape
    blocks = lax.axis_size("inp")
    devices = blocks * lax.axis_size("chan")
    frame_total = local_len // L * lax.axis_size("chan")
    spectra = channelize(voltages)
    spectra = spectra.reshape(devices, 2 * NCH // devices, spectra.shape[1])
    turned = lax.all_to_all(spectra, EVERY, 0, 0, tiled=True)
    tiles = all_tiles(turned, tile_table, blocks, width, frame_total)
    tiles = tiles.reshape(blocks, -1, tile_table.shape[0] // blocks, *tiles.shape[1:])
    out = widen(lax.all_to_all(tiles, "inp", 0, 0, tiled=True))
    return out.reshape(-1, *out.shape[2:])


def solution(mesh):
    return jax.shard_map(
        on_device,
        mesh=mesh,
        in_specs=(P("inp", "chan"), P()),
        out_specs=P("chan", "inp", None, None),
        check_vma=False,
    )
```

time: 197 us -> 186 us (0.944)
  Pallas kernels: 41.4 us -> 33.3 us
  waiting for transfers between devices: 29.7 us -> 25.7 us
    pallas_call x1, Pallas kernels: 15.4 us -> 10.2 us  [all_tiles(): pl.pallas_call(functools.partial(gram_kernel, float(frame_total)), name='...]
    all_to_all x1, waiting for transfers between devices: 29.7 us -> 25.7 us  [on_device(): turned = lax.all_to_all(spectra, EVERY, 0, 0, tiled=True)]
    pallas_call x3 -> x4, Pallas kernels: 26 us -> 23.1 us  [the longest x1 9.63 us: channelize(): pl.pallas_call(early_kernel, name='channelize_early', in_specs=[hbm] * 4,...]
  transfers between devices with their start and end apart: 2 -> 2, of which waited for: 1 -> 1; matrix products, arithmetic and copies ran while one was open for 0% -> 0% of each run, Pallas kernels for 6% -> 7%
where the time goes in v3:
time: 186 us; the launch traced here: 185 us
  blocking collectives  110 us (59%)
  Pallas kernels  33.3 us (18%)
  waiting for transfers between devices  25.7 us (14%)
  starting transfers between devices  14.3 us (8%)
  local copies, waits for them, and re-layouts  1.92 us (1%)
    all_to_all x1, blocking collectives, on_device(): out = widen(lax.all_to_all(tiles, 'inp', 0, 0, tiled=True))  110 us
    all_to_all x1, waiting for transfers between devices, on_device(): turned = lax.all_to_all(spectra, EVERY, 0, 0, tiled=True)  25.7 us
    all_to_all x1, starting transfers between devices, on_device(): turned = lax.all_to_all(spectra, EVERY, 0, 0, tiled=True)  13 us
    pallas_call x1, Pallas kernels, all_tiles(): pl.pallas_call(functools.partial(gram_kernel, float(frame_total)), name='...  10.2 us
    pallas_call x1, Pallas kernels, channelize(): pl.pallas_call(early_kernel, name='channelize_early', in_specs=[hbm] * 4,...  9.63 us
    pallas_call x1, Pallas kernels, widen(): pl.pallas_call(widen_kernel, name='widen', grid=(8,), in_specs=[pl.BlockS...  7 us
  transfers between devices with their start and end apart: 2, of which 1 were waited for; matrix products, arithmetic and copies ran while one was open for 0% of the time, Pallas kernels for 7%

profile of v3, /device:TPU:0, one launch (start us, length us, event | category | flops | bytes accessed | tf_op | source)
XLA Modules:
  0.0 185.4 jit_solution(5885821418889040437)
XLA Ops:
  0.0 1.2 slice.3
  1.2 1.3 collective-permute-start
  2.5 9.6 %channelize_early.1 = (bf16[1024,1024]{1,0:T(8,128)(2,1)}, bf16[1024,2048]{1,0:T(8,128)(2,1)S(1)}, bf16[64,8192]{1,0:T(8,128)(2,1)S(1)}, f32[4,2048]{1,0:T(4,128)S(1)}) custom-call(f32[64,128]{1,0:T(8,128)} %constant.6.clone.coarse_hbm, f32[64,1024]{1,0:T(8,128)} %constant.7.clone.fine_hbm, f32[4,2048]{1,0:T(4,128)} %constant.8.clone.window_hbm, ...), custom_call_target="tpu_custom_call" | custom-call | flops 3000000000 | bytes 12582912 | tf_op jit(solution)/shard_map/channelize_early/pallas_call | solution.py:162
  12.1 0.0 collective-permute-done.following
  12.1 3.1 %channelize_late.1 = bf16[1024,1024]{1,0:T(8,128)(2,1)} custom-call(bf16[1024,2048]{1,0:T(8,128)(2,1)S(1)} %get-tuple-element.9.table, f32[4,2048]{1,0:T(4,128)S(1)} %get-tuple-element.10.window, bf16[64,8192]{1,0:T(8,128)(2,1)S(1)} %get-tuple-element.11.last, bf16[64,6144]{1,0:T(8,128)(2,1)S(1)} %collective-permute-done.following, ...), custom_call_target="tpu_custom_call", output_to_operand_aliasing={{}: (4, {})} | custom-call | flops 1000000000 | bytes 6291456 | tf_op jit(solution)/shard_map/channelize_late/pallas_call | solution.py:186
  15.2 0.0 copy-start
  15.2 13.0 %all-to-all-start = ((bf16[128,8,1024]{2,1,0:T(8,128)(2,1)}), bf16[128,8,1024]{2,1,0:T(8,128)(2,1)S(1)}, u32[]{:S(2)}, u32[]{:S(2)}) async-start(bf16[128,8,1024]{2,1,0:T(8,128)(2,1)} %bitcast), calls=%async_computation | async-start | bytes 4194304 | tf_op jit(solution)/shard_map/all_to_all | solution.py:360
  28.2 0.0 copy-done
  28.2 0.7 copy.7.slots
  28.9 3.4 %places.1 = s32[18,16]{1,0:T(8,128)} custom-call(s32[144,2]{1,0:T(8,128)} %copy.7.slots), custom_call_target="tpu_custom_call" | custom-call | flops 1000000 | bytes 4096 | tf_op jit(solution)/shard_map/places/pallas_call | solution.py:218
  32.3 25.7 %all-to-all-done.spectra = bf16[128,8,1024]{2,1,0:T(8,128)(2,1)S(1)} async-done(((bf16[128,8,1024]{2,1,0:T(8,128)(2,1)}), bf16[128,8,1024]{2,1,0:T(8,128)(2,1)S(1)}, u32[]{:S(2)}, u32[]{:S(2)}) %all-to-all-start) | async-done | bytes 2097184 | tf_op jit(solution)/shard_map/all_to_all | solution.py:360
  58.0 10.2 %gram.1 = bf16[576,64,128]{2,1,0:T(8,128)(2,1)S(1)} custom-call(s32[18,16]{1,0:T(8,128)} %places.1, bf16[128,8,1024]{2,1,0:T(8,128)(2,1)S(1)} %all-to-all-done.spectra), custom_call_target="tpu_custom_call" | custom-call | flops 3000000000 | bytes 12582912 | tf_op jit(solution)/shard_map/gram/pallas_call | solution.py:311
  68.2 110.3 %all_to_all.10.tiles = bf16[16,4,9,64,128]{4,3,2,1,0:T(8,128)(2,1)S(1)} all-to-all(bf16[16,4,9,64,128]{4,3,2,1,0:T(8,128)(2,1)S(1)} %bitcast.3), channel_id=1, replica_groups=mesh['chan'=8,'inp'=16] {'inp'}, dimensions={0} | all-to-all | bytes 18874368 | tf_op jit(solution)/shard_map/all_to_all | solution.py:363
  178.4 7.0 %widen.1 = f32[16,4,9,64,128]{4,3,2,1,0:T(8,128)} custom-call(bf16[16,4,9,64,128]{4,3,2,1,0:T(8,128)(2,1)S(1)} %all_to_all.10.tiles), custom_call_target="tpu_custom_call" | custom-call | bytes 29360128 | tf_op jit(solution)/shard_map/widen/pallas_call | solution.py:341
Async XLA Ops:
  1.2 10.9 %collective-permute-start = (bf16[64,6144]{1,0:T(8,128)(2,1)S(1)}, bf16[64,6144]{1,0:T(8,128)(2,1)S(1)}, u32[]{:S(2)}, u32[]{:S(2)}) collective-permute-start(bf16[64,6144]{1,0:T(8,128)(2,1)S(1)} %slice.3), channel_id=1, source_target_pairs={{16,0},{32,16},{48,32},{64,48},{80,64},{96,80},{112,96},{17,1},{33... | collective-permute-start | bytes 2359304 | tf_op jit(solution)/shard_map/ppermute | solution.py:155
  15.2 13.0 %copy-start = (s32[144,2]{0,1:T(2,128)S(1)}, s32[144,2]{0,1:T(2,128)}, u32[]{:S(2)}) copy-start(s32[144,2]{0,1:T(2,128)} %param.6) | copy-start | bytes 3460
  15.2 42.7 %all-to-all-start = ((bf16[128,8,1024]{2,1,0:T(8,128)(2,1)}), bf16[128,8,1024]{2,1,0:T(8,128)(2,1)S(1)}, u32[]{:S(2)}, u32[]{:S(2)}) async-start(bf16[128,8,1024]{2,1,0:T(8,128)(2,1)} %bitcast), calls=%async_computation | async-start | bytes 4194304 | tf_op jit(solution)/shard_map/all_to_all | solution.py:360

commit v4 on v3

--- a/solution.py
+++ b/solution.py
@@ -70,15 +70,27 @@
             filtered[f * width + r : f * width + r + 16, at] = total.astype(jnp.bfloat16)
 
 
-def filter_frames(window, frames, filtered):
+def filter_frames(window, frames, filtered, beside=None, start=0):
     def column(j, carry):
         filter_column(window, frames, filtered, j)
-        return carry
-
-    lax.fori_loop(0, L // LANES, column, 0)
-
-
-def transform(table, filtered, spectra, beside=None):
+        return carry if beside is None else beside(j, carry)
+
+    return lax.fori_loop(0, L // LANES, column, start)
+
+
+def note_places(slots, places, channels, owner, empty):
+    blocks = L // LANES
+    per_owner = slots.shape[1] // blocks
+    for k in range(per_owner):
+        a, b = slots[0, owner * per_owner + k], slots[1, owner * per_owner + k]
+        place = owner * (channels * per_owner) + k
+        present = a >= 0
+        places[jnp.where(present, a * blocks + b, blocks * blocks + empty)] = place
+        empty = empty + jnp.where(present, 0, 1)
+    return empty
+
+
+def transform(table, filtered, spectra, columns, beside=None):
     rows = 512
     chunks = 2 * NCH // rows
     share = L // LANES // chunks
@@ -88,7 +100,7 @@
         product = lax.dot_general(
             table[at, :], filtered[...], (((1,), (1,)), ((), ())), preferred_element_type=jnp.float32
         )
-        spectra[at, :] = product.astype(jnp.bfloat16)
+        spectra[at, columns] = product.astype(jnp.bfloat16)
         if beside is not None:
             for j in range(share):
                 beside(i * share + j)
@@ -98,7 +110,8 @@
 
 
 def early_kernel(
-    coarse_hbm, fine_hbm, window_hbm, voltages, spectra, table, last, window, coarse, fine, head, even, odd, parts, sems, out_sems
+    channels, coarse_hbm, fine_hbm, window_hbm, voltages, slots, spectra, table, last, window, places,
+    coarse, fine, head, even, odd, sems,
 ):
     span = STEP * L
     width = even.shape[0]
@@ -115,38 +128,34 @@
     for copy in loads:
         copy.wait()
     build_table(coarse, fine, table)
-    places = [(head, f * L) for f in range((steps - 1) * STEP)] + [(last, f * L) for f in range(STEP)]
-    frames = lambda n: places[n * STEP : (n + 1) * STEP + TAPS - 1]
+    samples = [(head, f * L) for f in range((steps - 1) * STEP)] + [(last, f * L) for f in range(STEP)]
+    frames = lambda n: samples[n * STEP : (n + 1) * STEP + TAPS - 1]
     copies[0].wait()
     copies[1].wait()
     filtered = [even, odd]
-    filter_frames(window, frames(0), even)
-    outs = []
+    note = lambda j, empty: note_places(slots, places, channels, j, empty)
+    places[places.shape[0] - 1] = filter_frames(window, frames(0), even, note, 0)
     for n in range(steps - 1):
         beside = None
         if n < steps - 2:
             copies[n + 2].wait()
             beside = lambda j, n=n: filter_column(window, frames(n + 1), filtered[(n + 1) % 2], j)
-        transform(table, filtered[n % 2], parts.at[n], beside)
-        columns = spectra.at[:, n * width : (n + 1) * width]
-        outs.append(pltpu.make_async_copy(parts.at[n], columns, out_sems.at[n]))
-        outs[n].start()
-    for copy in outs:
-        copy.wait()
+        transform(table, filtered[n % 2], spectra, slice(n * width, (n + 1) * width), beside)
 
 
 def late_kernel(table, window, last, following, earlier, spectra, filtered):
     del earlier
     frames = [(last, f * L) for f in range(STEP)] + [(following, f * L) for f in range(TAPS - 1)]
     filter_frames(window, frames, filtered)
-    transform(table, filtered, spectra)
+    first = spectra.shape[1] - filtered.shape[0]
+    transform(table, filtered, spectra, slice(first, spectra.shape[1]))
 
 
 def in_hbm(array):
     return pltpu.with_memory_space_constraint(array, pltpu.HBM)
 
 
-def channelize(voltages):
+def channelize(voltages, tile_table, blocks, channels):
     width, local_len = voltages.shape
     steps = local_len // (STEP * L)
     span = STEP * L
@@ -154,21 +163,24 @@
     devices = lax.axis_size("chan")
     following = lax.ppermute(voltages[:, :halo], "chan", [(i, i - 1) for i in range(1, devices)])
     constants = [*twiddle_factors(), filter_window()]
+    assert blocks == L // LANES
     columns = STEP * width
     here = pl.BlockSpec(memory_space=pltpu.VMEM)
     hbm = pl.BlockSpec(memory_space=pltpu.HBM)
     spectra_shape = jax.ShapeDtypeStruct((2 * NCH, steps * columns), jnp.bfloat16)
     filtered = pltpu.VMEM((columns, L), jnp.bfloat16)
-    early, table, last, window = pl.pallas_call(
-        early_kernel,
+    smem = pl.BlockSpec(memory_space=pltpu.SMEM)
+    early, table, last, window, places = pl.pallas_call(
+        functools.partial(early_kernel, channels),
         name="channelize_early",
-        in_specs=[hbm] * 4,
-        out_specs=[hbm, here, here, here],
+        in_specs=[hbm] * 4 + [smem],
+        out_specs=[here] * 4 + [smem],
         out_shape=[
             spectra_shape,
             jax.ShapeDtypeStruct((2 * NCH, L), jnp.bfloat16),
             jax.ShapeDtypeStruct((width, span), jnp.bfloat16),
             jax.ShapeDtypeStruct((TAPS, L), jnp.float32),
+            jax.ShapeDtypeStruct((blocks * blocks + tile_table.shape[0] + 1,), jnp.int32),
         ],
         scratch_shapes=[
             pltpu.VMEM(constants[0].shape, jnp.float32),
@@ -176,53 +188,23 @@
             pltpu.VMEM((width, local_len - span), jnp.bfloat16),
             filtered,
             filtered,
-            pltpu.VMEM((steps - 1, 2 * NCH, columns), jnp.bfloat16),
             pltpu.SemaphoreType.DMA((3 + steps,)),
-            pltpu.SemaphoreType.DMA((steps - 1,)),
         ],
         compiler_params=pltpu.CompilerParams(vmem_limit_bytes=24 * 2**20),
         cost_estimate=pl.CostEstimate(flops=3 * 10**9, bytes_accessed=12 * 2**20, transcendentals=0),
-    )(*(in_hbm(jnp.asarray(t)) for t in constants), in_hbm(voltages))
-    return pl.pallas_call(
+    )(*(in_hbm(jnp.asarray(t)) for t in constants), in_hbm(voltages), tile_table.T)
+    spectra = pl.pallas_call(
         late_kernel,
         name="channelize_late",
-        grid=(1,),
-        in_specs=[here] * 4 + [pl.BlockSpec(memory_space=pl.ANY)],
-        out_specs=pl.BlockSpec((2 * NCH, columns), lambda j: (0, steps - 1)),
+        in_specs=[here] * 5,
+        out_specs=here,
         out_shape=spectra_shape,
         scratch_shapes=[filtered],
         input_output_aliases={4: 0},
         compiler_params=pltpu.CompilerParams(vmem_limit_bytes=24 * 2**20),
         cost_estimate=pl.CostEstimate(flops=10**9, bytes_accessed=6 * 2**20, transcendentals=0),
     )(table, window, last, following, early)
-
-
-def places_kernel(channels, slots, places):
-    blocks = places.shape[1]
-    per_owner = slots.shape[0] // blocks
-
-    def owner_slots(owner, empty):
-        for k in range(per_owner):
-            a, b = slots[owner * per_owner + k, 0], slots[owner * per_owner + k, 1]
-            present = a >= 0
-            row = jnp.where(present, a, blocks + 1)
-            column = jnp.where(present, b, empty)
-            places[row, column] = owner * (channels * per_owner) + k
-            empty = empty + jnp.where(present, 0, 1)
-        return empty
-
-    places[blocks, 0] = lax.fori_loop(0, blocks, owner_slots, 0)
-
-
-def slot_places(tile_table, blocks, channels):
-    return pl.pallas_call(
-        functools.partial(places_kernel, channels),
-        name="places",
-        in_specs=[pl.BlockSpec(memory_space=pltpu.SMEM)],
-        out_specs=pl.BlockSpec(memory_space=pltpu.SMEM),
-        out_shape=jax.ShapeDtypeStruct((blocks + 2, blocks), jnp.int32),
-        cost_estimate=pl.CostEstimate(flops=10**6, bytes_accessed=2**12, transcendentals=0),
-    )(tile_table)
+    return spectra, places
 
 
 def gram_kernel(frame_total, places, spectra, tiles, wide, lefts, rights, row_scale, col_scale):
@@ -251,10 +233,10 @@
 
         def clear(n, carry):
             for c in range(channels):
-                tiles[places[blocks + 1, n] + c * per_owner] = jnp.zeros((width, LANES), jnp.bfloat16)
+                tiles[places[blocks * blocks + n] + c * per_owner] = jnp.zeros((width, LANES), jnp.bfloat16)
             return carry
 
-        lax.fori_loop(0, places[blocks, 0], clear, 0)
+        lax.fori_loop(0, places[places.shape[0] - 1], clear, 0)
 
     low = lax.broadcasted_iota(jnp.int32, (depth, LANES), 1) < width
     turn = lambda x: pltpu.roll(x, LANES // 2, 1)
@@ -267,6 +249,8 @@
         for n in range(2):
             re = wide[2 * q + n, pl.ds(2 * channel, depth, stride=parts), :]
             im = wide[2 * q + n, pl.ds(2 * channel + 1, depth, stride=parts), :]
+            power = jnp.sum(re * re + im * im, axis=0, keepdims=True)
+            re, im = re.astype(jnp.bfloat16), im.astype(jnp.bfloat16)
             re_turned, im_turned = turn(re), turn(im)
             pair.append((re, re_turned, im, im_turned))
             lanes = slice(n * LANES, (n + 1) * LANES)
@@ -277,12 +261,11 @@
                 jnp.where(low, im_turned, re),
             )
             for k, part in enumerate(right):
-                rights[q, k * depth : (k + 1) * depth, lanes] = part.astype(jnp.bfloat16)
-            power = jnp.sum(re * re + im * im, axis=0, keepdims=True)
+                rights[q, k * depth : (k + 1) * depth, lanes] = part
             col_scale[q, :, lanes] = scale(power + turn(power))
         x, y = pair
         flat = [jnp.where(low, x[k], y[k ^ 1]) for k in range(4)]
-        flat = jnp.concatenate(flat, axis=0).astype(jnp.bfloat16).T
+        flat = jnp.concatenate(flat, axis=0).T
         rows = pl.ds(pl.multiple_of(q * LANES, LANES), LANES)
         lefts[rows, :] = flat
         flat = flat.astype(jnp.float32)
@@ -299,15 +282,14 @@
         for n in range(2):
             for a in range(2 * q + n + 1):
                 tile = product[a * width : (a + 1) * width, n * LANES : (n + 1) * LANES]
-                tiles[places[a, 2 * q + n] + offset] = tile
-
-
-def all_tiles(spectra, tile_table, blocks, width, frame_total):
+                tiles[places[a * blocks + 2 * q + n] + offset] = tile
+
+
+def all_tiles(spectra, places, per_owner, blocks, width, frame_total):
     parts = spectra.shape[1]
     channels = parts // 2
     times = spectra.shape[0] // blocks
     depth = times * spectra.shape[2] // LANES
-    per_owner = tile_table.shape[0] // blocks
     return pl.pallas_call(
         functools.partial(gram_kernel, float(frame_total)),
         name="gram",
@@ -327,7 +309,7 @@
         out_shape=jax.ShapeDtypeStruct((blocks * channels * per_owner, width, 2 * width), jnp.bfloat16),
         compiler_params=pltpu.CompilerParams(vmem_limit_bytes=32 * 2**20),
         cost_estimate=pl.CostEstimate(flops=3 * 10**9, bytes_accessed=12 * 2**20, transcendentals=0),
-    )(in_hbm(slot_places(tile_table, blocks, channels)), spectra)
+    )(places, spectra)
 
 
 def widen_kernel(tiles, out):
@@ -355,11 +337,13 @@
     blocks = lax.axis_size("inp")
     devices = blocks * lax.axis_size("chan")
     frame_total = local_len // L * lax.axis_size("chan")
-    spectra = channelize(voltages)
-    spectra = spectra.reshape(devices, 2 * NCH // devices, spectra.shape[1])
+    channels = NCH // devices
+    per_owner = tile_table.shape[0] // blocks
+    spectra, places = channelize(voltages, tile_table, blocks, channels)
+    spectra = spectra.reshape(devices, 2 * channels, spectra.shape[1])
     turned = lax.all_to_all(spectra, EVERY, 0, 0, tiled=True)
-    tiles = all_tiles(turned, tile_table, blocks, width, frame_total)
-    tiles = tiles.reshape(blocks, -1, tile_table.shape[0] // blocks, *tiles.shape[1:])
+    tiles = all_tiles(turned, places, per_owner, blocks, width, frame_total)
+    tiles = tiles.reshape(blocks, channels, per_owner, *tiles.shape[1:])
     out = widen(lax.all_to_all(tiles, "inp", 0, 0, tiled=True))
     return out.reshape(-1, *out.shape[2:])
 

time: 186 us -> 184 us (0.989)
  blocking collectives: 110 us -> 152 us
  waiting for transfers between devices: 25.7 us -> 0.01 us
  starting transfers between devices: 14.3 us -> 1.29 us
  Pallas kernels: 33.3 us -> 28.8 us
    all_to_all x0 -> x1, blocking collectives: none -> 41.5 us  [on_device(): turned = lax.all_to_all(spectra, EVERY, 0, 0, tiled=True)]
    all_to_all x1 -> x0, waiting for transfers between devices: 25.7 us -> none  [on_device(): turned = lax.all_to_all(spectra, EVERY, 0, 0, tiled=True)]
    all_to_all x1 -> x0, starting transfers between devices: 13 us -> none  [on_device(): turned = lax.all_to_all(spectra, EVERY, 0, 0, tiled=True)]
    pallas_call x3 -> x2, Pallas kernels: 16.1 us -> 12.3 us  [the longest x1 9.94 us: channelize(): pl.pallas_call(functools.partial(early_kernel, channels), name='channeliz...]
  transfers between devices with their start and end apart: 2 -> 1, of which waited for: 1 -> 0; matrix products, arithmetic and copies ran while one was open for 0% -> 0% of each run, Pallas kernels for 7% -> 5%
where the time goes in v4:
time: 184 us
  blocking collectives  152 us (83%)
  Pallas kernels  28.8 us (16%)
  local copies, waits for them, and re-layouts  1.86 us (1%)
    all_to_all x1, blocking collectives, on_device(): out = widen(lax.all_to_all(tiles, 'inp', 0, 0, tiled=True))  110 us
    all_to_all x1, blocking collectives, on_device(): turned = lax.all_to_all(spectra, EVERY, 0, 0, tiled=True)  41.5 us
    pallas_call x1, Pallas kernels, channelize(): pl.pallas_call(functools.partial(early_kernel, channels), name='channeliz...  9.94 us
    pallas_call x1, Pallas kernels, all_tiles(): pl.pallas_call(functools.partial(gram_kernel, float(frame_total)), name='...  9.54 us
    pallas_call x1, Pallas kernels, widen(): pl.pallas_call(widen_kernel, name='widen', grid=(8,), in_specs=[pl.BlockS...  7 us
  transfers between devices with their start and end apart: 1, of which 0 were waited for; matrix products, arithmetic and copies ran while one was open for 0% of the time, Pallas kernels for 5%

profile of v4, /device:TPU:0, one launch (start us, length us, event | category | flops | bytes accessed | tf_op | source)
XLA Modules:
  0.0 183.8 jit_solution(1833867414019719705)
XLA Ops:
  0.0 1.2 slice.3
  1.2 1.3 collective-permute-start
  2.5 0.0 copy-start
  2.5 0.7 copy-done
  3.2 9.9 %channelize_early.1 = (bf16[1024,1024]{1,0:T(8,128)(2,1)S(1)}, bf16[1024,2048]{1,0:T(8,128)(2,1)S(1)}, bf16[64,8192]{1,0:T(8,128)(2,1)S(1)}, f32[4,2048]{1,0:T(4,128)S(1)}, s32[401]{0:T(512)S(1)}) custom-call(f32[64,128]{1,0:T(8,128)} %constant.6.clone.coarse_hbm, f32[64,1024]{1,0:T(8,128)} %constant.7.clone.fine_hbm, f32[4,2048]{1,0:T(4,128)} %constant.8.clone.window_hbm, ...), custom_call_target="tpu_custom_call" | custom-call | flops 3000000000 | bytes 12582912 | tf_op jit(solution)/shard_map/channelize_early/pallas_call | solution.py:173
  13.1 0.0 collective-permute-done.following
  13.1 2.3 %channelize_late.1 = bf16[1024,1024]{1,0:T(8,128)(2,1)S(1)} custom-call(bf16[1024,2048]{1,0:T(8,128)(2,1)S(1)} %get-tuple-element.11.table, f32[4,2048]{1,0:T(4,128)S(1)} %get-tuple-element.12.window, bf16[64,8192]{1,0:T(8,128)(2,1)S(1)} %get-tuple-element.13.last, ...), custom_call_target="tpu_custom_call", output_to_operand_aliasing={{}: (4, {})} | custom-call | flops 1000000000 | bytes 6291456 | tf_op jit(solution)/shard_map/channelize_late/pallas_call | solution.py:196
  15.5 41.5 %all_to_all.10.spectra = bf16[128,8,1024]{2,1,0:T(8,128)(2,1)S(1)} all-to-all(bf16[128,8,1024]{2,1,0:T(8,128)(2,1)S(1)} %bitcast.5), channel_id=1, replica_groups=mesh['chan'=8,'inp'=16] {'chan','inp'}, dimensions={0} | all-to-all | bytes 4194304 | tf_op jit(solution)/shard_map/all_to_all | solution.py:344
  57.0 9.5 %gram.1 = bf16[576,64,128]{2,1,0:T(8,128)(2,1)S(1)} custom-call(s32[401]{0:T(512)S(1)} %get-tuple-element.10.places, bf16[128,8,1024]{2,1,0:T(8,128)(2,1)S(1)} %all_to_all.10.spectra), custom_call_target="tpu_custom_call" | custom-call | flops 3000000000 | bytes 12582912 | tf_op jit(solution)/shard_map/gram/pallas_call | solution.py:293
  66.6 110.3 %all_to_all.11.tiles = bf16[16,4,9,64,128]{4,3,2,1,0:T(8,128)(2,1)S(1)} all-to-all(bf16[16,4,9,64,128]{4,3,2,1,0:T(8,128)(2,1)S(1)} %bitcast.4), channel_id=1, replica_groups=mesh['chan'=8,'inp'=16] {'inp'}, dimensions={0} | all-to-all | bytes 18874368 | tf_op jit(solution)/shard_map/all_to_all | solution.py:347
  176.8 7.0 %widen.1 = f32[16,4,9,64,128]{4,3,2,1,0:T(8,128)} custom-call(bf16[16,4,9,64,128]{4,3,2,1,0:T(8,128)(2,1)S(1)} %all_to_all.11.tiles), custom_call_target="tpu_custom_call" | custom-call | bytes 29360128 | tf_op jit(solution)/shard_map/widen/pallas_call | solution.py:323
Async XLA Ops:
  1.2 11.9 %collective-permute-start = (bf16[64,6144]{1,0:T(8,128)(2,1)S(1)}, bf16[64,6144]{1,0:T(8,128)(2,1)S(1)}, u32[]{:S(2)}, u32[]{:S(2)}) collective-permute-start(bf16[64,6144]{1,0:T(8,128)(2,1)S(1)} %slice.3), channel_id=1, source_target_pairs={{16,0},{32,16},{48,32},{64,48},{80,64},{96,80},{112,96},{17,1},{33... | collective-permute-start | bytes 2359304 | tf_op jit(solution)/shard_map/ppermute | solution.py:164
  2.5 0.7 copy-start

commit v5 on v4

--- a/solution.py
+++ b/solution.py
@@ -70,6 +70,38 @@
             filtered[f * width + r : f * width + r + 16, at] = total.astype(jnp.bfloat16)
 
 
+def start_column(window, last, partial, j):
+    at = pl.ds(pl.multiple_of(j * LANES, LANES), LANES)
+    taps = [window[k : k + 1, at] for k in range(TAPS)]
+    for r in range(0, last.shape[0], 16):
+        rows = slice(r, r + 16)
+        samples = [
+            last[rows, pl.ds(pl.multiple_of(f * L + j * LANES, LANES), LANES)].astype(jnp.float32) for f in range(STEP)
+        ]
+        for f in range(STEP):
+            total = samples[f] * taps[0]
+            for k in range(1, STEP - f):
+                total = total + samples[f + k] * taps[k]
+            partial[f, rows, at] = total
+
+
+def finish_column(window, partial, following, filtered, j):
+    width = partial.shape[1]
+    at = pl.ds(pl.multiple_of(j * LANES, LANES), LANES)
+    taps = [window[k : k + 1, at] for k in range(TAPS)]
+    for r in range(0, width, 16):
+        rows = slice(r, r + 16)
+        samples = [
+            following[rows, pl.ds(pl.multiple_of(f * L + j * LANES, LANES), LANES)].astype(jnp.float32)
+            for f in range(TAPS - 1)
+        ]
+        for f in range(STEP):
+            total = partial[f, rows, at]
+            for k in range(STEP - f, TAPS):
+                total = total + samples[f + k - STEP] * taps[k]
+            filtered[f * width + r : f * width + r + 16, at] = total.astype(jnp.bfloat16)
+
+
 def filter_frames(window, frames, filtered, beside=None, start=0):
     def column(j, carry):
         filter_column(window, frames, filtered, j)
@@ -110,13 +142,13 @@
 
 
 def early_kernel(
-    channels, coarse_hbm, fine_hbm, window_hbm, voltages, slots, spectra, table, last, window, places,
-    coarse, fine, head, even, odd, sems,
+    channels, coarse_hbm, fine_hbm, window_hbm, slots_hbm, voltages, spectra, table, partial, window, places,
+    coarse, fine, head, last, even, odd, slots, sems,
 ):
     span = STEP * L
     width = even.shape[0]
     steps = spectra.shape[1] // width
-    small = [(coarse_hbm, coarse), (fine_hbm, fine), (window_hbm, window)]
+    small = [(coarse_hbm, coarse), (fine_hbm, fine), (window_hbm, window), (slots_hbm, slots)]
     loads = [pltpu.make_async_copy(source, target, sems.at[n]) for n, (source, target) in enumerate(small)]
     copies = []
     for n in range(steps):
@@ -142,13 +174,29 @@
             beside = lambda j, n=n: filter_column(window, frames(n + 1), filtered[(n + 1) % 2], j)
         transform(table, filtered[n % 2], spectra, slice(n * width, (n + 1) * width), beside)
 
-
-def late_kernel(table, window, last, following, earlier, spectra, filtered):
+    def column(j, carry):
+        start_column(window, last, partial, j)
+        return carry
+
+    lax.fori_loop(0, L // LANES, column, 0)
+
+
+def late_kernel(table, window, partial, following, earlier, spectra, filtered):
     del earlier
-    frames = [(last, f * L) for f in range(STEP)] + [(following, f * L) for f in range(TAPS - 1)]
-    filter_frames(window, frames, filtered)
+
+    def column(j, carry):
+        finish_column(window, partial, following, filtered, j)
+        return carry
+
+    lax.fori_loop(0, L // LANES, column, 0)
     first = spectra.shape[1] - filtered.shape[0]
     transform(table, filtered, spectra, slice(first, spectra.shape[1]))
+
+
+def halo_kernel(voltages, halo, sem):
+    copy = pltpu.make_async_copy(voltages.at[:, : halo.shape[1]], halo, sem)
+    copy.start()
+    copy.wait()
 
 
 def in_hbm(array):
@@ -161,24 +209,33 @@
     span = STEP * L
     halo = (TAPS - 1) * L
     devices = lax.axis_size("chan")
-    following = lax.ppermute(voltages[:, :halo], "chan", [(i, i - 1) for i in range(1, devices)])
+    here = pl.BlockSpec(memory_space=pltpu.VMEM)
+    hbm = pl.BlockSpec(memory_space=pltpu.HBM)
+    first = pl.pallas_call(
+        halo_kernel,
+        name="halo",
+        in_specs=[hbm],
+        out_specs=here,
+        out_shape=jax.ShapeDtypeStruct((width, halo), jnp.bfloat16),
+        scratch_shapes=[pltpu.SemaphoreType.DMA],
+        compiler_params=pltpu.CompilerParams(vmem_limit_bytes=2**20),
+    )(in_hbm(voltages))
+    following = lax.ppermute(first, "chan", [(i, i - 1) for i in range(1, devices)])
     constants = [*twiddle_factors(), filter_window()]
     assert blocks == L // LANES
     columns = STEP * width
-    here = pl.BlockSpec(memory_space=pltpu.VMEM)
-    hbm = pl.BlockSpec(memory_space=pltpu.HBM)
     spectra_shape = jax.ShapeDtypeStruct((2 * NCH, steps * columns), jnp.bfloat16)
     filtered = pltpu.VMEM((columns, L), jnp.bfloat16)
     smem = pl.BlockSpec(memory_space=pltpu.SMEM)
-    early, table, last, window, places = pl.pallas_call(
+    early, table, partial, window, places = pl.pallas_call(
         functools.partial(early_kernel, channels),
         name="channelize_early",
-        in_specs=[hbm] * 4 + [smem],
+        in_specs=[hbm] * 5,
         out_specs=[here] * 4 + [smem],
         out_shape=[
             spectra_shape,
             jax.ShapeDtypeStruct((2 * NCH, L), jnp.bfloat16),
-            jax.ShapeDtypeStruct((width, span), jnp.bfloat16),
+            jax.ShapeDtypeStruct((STEP, width, L), jnp.float32),
             jax.ShapeDtypeStruct((TAPS, L), jnp.float32),
             jax.ShapeDtypeStruct((blocks * blocks + tile_table.shape[0] + 1,), jnp.int32),
         ],
@@ -186,13 +243,15 @@
             pltpu.VMEM(constants[0].shape, jnp.float32),
             pltpu.VMEM(constants[1].shape, jnp.float32),
             pltpu.VMEM((width, local_len - span), jnp.bfloat16),
+            pltpu.VMEM((width, span), jnp.bfloat16),
             filtered,
             filtered,
-            pltpu.SemaphoreType.DMA((3 + steps,)),
+            pltpu.SMEM(tile_table.shape[::-1], jnp.int32),
+            pltpu.SemaphoreType.DMA((4 + steps,)),
         ],
         compiler_params=pltpu.CompilerParams(vmem_limit_bytes=24 * 2**20),
         cost_estimate=pl.CostEstimate(flops=3 * 10**9, bytes_accessed=12 * 2**20, transcendentals=0),
-    )(*(in_hbm(jnp.asarray(t)) for t in constants), in_hbm(voltages), tile_table.T)
+    )(*(in_hbm(jnp.asarray(t)) for t in constants), in_hbm(tile_table.T), in_hbm(voltages))
     spectra = pl.pallas_call(
         late_kernel,
         name="channelize_late",
@@ -203,7 +262,7 @@
         input_output_aliases={4: 0},
         compiler_params=pltpu.CompilerParams(vmem_limit_bytes=24 * 2**20),
         cost_estimate=pl.CostEstimate(flops=10**9, bytes_accessed=6 * 2**20, transcendentals=0),
-    )(table, window, last, following, early)
+    )(table, window, partial, following, early)
     return spectra, places
 
 
@@ -245,7 +304,7 @@
         return lax.rsqrt(power / frame_total + 1e-6)
 
     def build(q, carry):
-        pair = []
+        pair, factors = [], []
         for n in range(2):
             re = wide[2 * q + n, pl.ds(2 * channel, depth, stride=parts), :]
             im = wide[2 * q + n, pl.ds(2 * channel + 1, depth, stride=parts), :]
@@ -262,27 +321,31 @@
             )
             for k, part in enumerate(right):
                 rights[q, k * depth : (k + 1) * depth, lanes] = part
-            col_scale[q, :, lanes] = scale(power + turn(power))
+            factor = scale(power + turn(power))
+            col_scale[q, :, lanes] = factor
+            factors.append(factor)
         x, y = pair
         flat = [jnp.where(low, x[k], y[k ^ 1]) for k in range(4)]
         flat = jnp.concatenate(flat, axis=0).T
         rows = pl.ds(pl.multiple_of(q * LANES, LANES), LANES)
         lefts[rows, :] = flat
-        flat = flat.astype(jnp.float32)
-        row_scale[rows, :] = scale(jnp.sum(flat * flat, axis=1, keepdims=True)) / frame_total
+        factor = jnp.where(low[:1], factors[0], factors[1]) / frame_total
+        row_scale[rows, :] = jnp.broadcast_to(factor, (8, LANES)).T[:, :1]
         return carry
 
     lax.fori_loop(0, blocks // 2, build, 0, unroll=2)
 
     offset = channel * per_owner
     for q in range(blocks // 2):
-        rows = (q + 1) * LANES
-        product = jnp.dot(lefts[:rows, :], rights[q], preferred_element_type=jnp.float32)
-        product = (product * row_scale[:rows, :] * col_scale[q]).astype(jnp.bfloat16)
-        for n in range(2):
-            for a in range(2 * q + n + 1):
-                tile = product[a * width : (a + 1) * width, n * LANES : (n + 1) * LANES]
-                tiles[places[a * blocks + 2 * q + n] + offset] = tile
+        for first in range(0, (q + 1) * LANES, 256):
+            rows = slice(first, min(first + 256, (q + 1) * LANES))
+            product = jnp.dot(lefts[rows, :], rights[q], preferred_element_type=jnp.float32)
+            product = (product * row_scale[rows, :] * col_scale[q]).astype(jnp.bfloat16)
+            for n in range(2):
+                for a in range(rows.start // width, min(rows.stop // width, 2 * q + n + 1)):
+                    start = a * width - rows.start
+                    tile = product[start : start + width, n * LANES : (n + 1) * LANES]
+                    tiles[places[a * blocks + 2 * q + n] + offset] = tile
 
 
 def all_tiles(spectra, places, per_owner, blocks, width, frame_total):
@@ -312,21 +375,40 @@
     )(places, spectra)
 
 
-def widen_kernel(tiles, out):
-    out[...] = tiles[...].astype(jnp.float32)
+def widen_kernel(tiles, out, held, sems):
+    sources, channels = tiles.shape[:2]
+    buffers = held.shape[0]
+    copy = lambda d, n: pltpu.make_async_copy(held.at[n], out.at[d], sems.at[n])
+
+    def source(d, carry):
+        n = lax.rem(d, buffers)
+
+        @pl.when(d >= buffers)
+        def _():
+            copy(d - buffers, n).wait()
+
+        def channel(c, carry):
+            held[n, c] = tiles[d, c].astype(jnp.float32)
+            return carry
+
+        lax.fori_loop(0, channels, channel, 0)
+        copy(d, n).start()
+        return carry
+
+    lax.fori_loop(0, sources, source, 0)
+    for d in range(sources - buffers, sources):
+        copy(d, d % buffers).wait()
 
 
 def widen(tiles):
-    sources, channels, per_owner, width, lanes = tiles.shape
-    block = (sources // 8, channels, per_owner, width, lanes)
-    at = lambda d: (d, 0, 0, 0, 0)
+    buffers = 8
     return pl.pallas_call(
         widen_kernel,
         name="widen",
-        grid=(8,),
-        in_specs=[pl.BlockSpec(block, at)],
-        out_specs=pl.BlockSpec(block, at),
+        in_specs=[pl.BlockSpec(memory_space=pltpu.VMEM)],
+        out_specs=pl.BlockSpec(memory_space=pltpu.HBM),
         out_shape=jax.ShapeDtypeStruct(tiles.shape, jnp.float32),
+        scratch_shapes=[pltpu.VMEM((buffers, *tiles.shape[1:]), jnp.float32), pltpu.SemaphoreType.DMA((buffers,))],
         compiler_params=pltpu.CompilerParams(vmem_limit_bytes=24 * 2**20),
         cost_estimate=pl.CostEstimate(flops=0, bytes_accessed=28 * 2**20, transcendentals=0),
     )(tiles)

time: 184 us -> 182 us (0.989)
  local copies, waits for them, and re-layouts: 1.86 us -> 0 us
    pallas_call x1 -> x2, Pallas kernels: 7 us -> 7.77 us  [the longest x1 6.63 us: widen(): pl.pallas_call(widen_kernel, name='widen', in_specs=[pl.BlockSpec(memory_...]
  transfers between devices with their start and end apart: 1 -> 1, of which waited for: 0 -> 0; matrix products, arithmetic and copies ran while one was open for 0% -> 0% of each run, Pallas kernels for 5% -> 6%
where the time goes in v5:
time: 182 us
  blocking collectives  152 us (84%)
  Pallas kernels  28.5 us (16%)
    all_to_all x1, blocking collectives, on_device(): out = widen(lax.all_to_all(tiles, 'inp', 0, 0, tiled=True))  110 us
    all_to_all x1, blocking collectives, on_device(): turned = lax.all_to_all(spectra, EVERY, 0, 0, tiled=True)  41.8 us
    pallas_call x1, Pallas kernels, channelize(): pl.pallas_call(functools.partial(early_kernel, channels), name='channeliz...  10.3 us
    pallas_call x1, Pallas kernels, all_tiles(): pl.pallas_call(functools.partial(gram_kernel, float(frame_total)), name='...  8.32 us
    pallas_call x1, Pallas kernels, widen(): pl.pallas_call(widen_kernel, name='widen', in_specs=[pl.BlockSpec(memory_...  6.63 us
  transfers between devices with their start and end apart: 1, of which 0 were waited for; matrix products, arithmetic and copies ran while one was open for 0% of the time, Pallas kernels for 6%

profile of v5, /device:TPU:0, one launch (start us, length us, event | category | flops | bytes accessed | tf_op | source)
XLA Modules:
  0.0 182.0 jit_solution(7729676849162838124)
XLA Ops:
  0.0 1.1 halo.1
  1.1 1.3 collective-permute-start
  2.4 10.3 %channelize_early.1 = (bf16[1024,1024]{1,0:T(8,128)(2,1)S(1)}, bf16[1024,2048]{1,0:T(8,128)(2,1)S(1)}, f32[4,64,2048]{2,1,0:T(8,128)S(1)}, f32[4,2048]{1,0:T(4,128)S(1)}, s32[401]{0:T(512)S(1)}) custom-call(f32[64,128]{1,0:T(8,128)} %constant.6.clone.coarse_hbm, f32[64,1024]{1,0:T(8,128)} %constant.7.clone.fine_hbm, f32[4,2048]{1,0:T(4,128)} %constant.8.clone.window_hbm, ...), custom_call_target="tpu_custom_call" | custom-call | flops 3000000000 | bytes 12582912 | tf_op jit(solution)/shard_map/channelize_early/pallas_call | solution.py:230
  12.8 0.0 collective-permute-done.following
  12.8 2.1 %channelize_late.1 = bf16[1024,1024]{1,0:T(8,128)(2,1)S(1)} custom-call(bf16[1024,2048]{1,0:T(8,128)(2,1)S(1)} %get-tuple-element.11.table, f32[4,2048]{1,0:T(4,128)S(1)} %get-tuple-element.12.window, f32[4,64,2048]{2,1,0:T(8,128)S(1)} %get-tuple-element.13.partial, ...), custom_call_target="tpu_custom_call", output_to_operand_aliasing={{}: (4, {})} | custom-call | flops 1000000000 | bytes 6291456 | tf_op jit(solution)/shard_map/channelize_late/pallas_call | solution.py:255
  14.9 41.8 %all_to_all.10.spectra = bf16[128,8,1024]{2,1,0:T(8,128)(2,1)S(1)} all-to-all(bf16[128,8,1024]{2,1,0:T(8,128)(2,1)S(1)} %bitcast.5), channel_id=1, replica_groups=mesh['chan'=8,'inp'=16] {'chan','inp'}, dimensions={0} | all-to-all | bytes 4194304 | tf_op jit(solution)/shard_map/all_to_all | solution.py:426
  56.7 8.3 %gram.1 = bf16[576,64,128]{2,1,0:T(8,128)(2,1)S(1)} custom-call(s32[401]{0:T(512)S(1)} %get-tuple-element.10.places, bf16[128,8,1024]{2,1,0:T(8,128)(2,1)S(1)} %all_to_all.10.spectra), custom_call_target="tpu_custom_call" | custom-call | flops 3000000000 | bytes 12582912 | tf_op jit(solution)/shard_map/gram/pallas_call | solution.py:356
  65.1 110.3 %all_to_all.11.tiles = bf16[16,4,9,64,128]{4,3,2,1,0:T(8,128)(2,1)S(1)} all-to-all(bf16[16,4,9,64,128]{4,3,2,1,0:T(8,128)(2,1)S(1)} %bitcast.4), channel_id=1, replica_groups=mesh['chan'=8,'inp'=16] {'inp'}, dimensions={0} | all-to-all | bytes 18874368 | tf_op jit(solution)/shard_map/all_to_all | solution.py:429
  175.3 6.6 %widen.1 = f32[16,4,9,64,128]{4,3,2,1,0:T(8,128)} custom-call(bf16[16,4,9,64,128]{4,3,2,1,0:T(8,128)(2,1)S(1)} %all_to_all.11.tiles), custom_call_target="tpu_custom_call" | custom-call | bytes 29360128 | tf_op jit(solution)/shard_map/widen/pallas_call | solution.py:405
Async XLA Ops:
  1.1 11.7 %collective-permute-start = (bf16[64,6144]{1,0:T(8,128)(2,1)S(1)}, bf16[64,6144]{1,0:T(8,128)(2,1)S(1)}, u32[]{:S(2)}, u32[]{:S(2)}) collective-permute-start(bf16[64,6144]{1,0:T(8,128)(2,1)S(1)} %halo.1), channel_id=1, source_target_pairs={{16,0},{32,16},{48,32},{64,48},{80,64},{96,80},{112,96},{17,1},{33... | collective-permute-start | bytes 2359304 | tf_op jit(solution)/shard_map/ppermute | solution.py:223

commit v6 on v5

--- a/solution.py
+++ b/solution.py
@@ -330,7 +330,7 @@
         rows = pl.ds(pl.multiple_of(q * LANES, LANES), LANES)
         lefts[rows, :] = flat
         factor = jnp.where(low[:1], factors[0], factors[1]) / frame_total
-        row_scale[rows, :] = jnp.broadcast_to(factor, (8, LANES)).T[:, :1]
+        row_scale[rows, :] = jnp.broadcast_to(factor, (LANES, LANES)).T
         return carry
 
     lax.fori_loop(0, blocks // 2, build, 0, unroll=2)
@@ -340,12 +340,12 @@
         for first in range(0, (q + 1) * LANES, 256):
             rows = slice(first, min(first + 256, (q + 1) * LANES))
             product = jnp.dot(lefts[rows, :], rights[q], preferred_element_type=jnp.float32)
-            product = (product * row_scale[rows, :] * col_scale[q]).astype(jnp.bfloat16)
             for n in range(2):
+                lanes = slice(n * LANES, (n + 1) * LANES)
+                part = (product[:, lanes] * row_scale[rows, :] * col_scale[q, :, lanes]).astype(jnp.bfloat16)
                 for a in range(rows.start // width, min(rows.stop // width, 2 * q + n + 1)):
                     start = a * width - rows.start
-                    tile = product[start : start + width, n * LANES : (n + 1) * LANES]
-                    tiles[places[a * blocks + 2 * q + n] + offset] = tile
+                    tiles[places[a * blocks + 2 * q + n] + offset] = part[start : start + width, :]
 
 
 def all_tiles(spectra, places, per_owner, blocks, width, frame_total):
@@ -365,7 +365,7 @@
                 pltpu.VMEM((blocks, depth * parts, LANES), jnp.float32),
                 pltpu.VMEM((blocks * width, 4 * depth), jnp.bfloat16),
                 pltpu.VMEM((blocks // 2, 4 * depth, 2 * LANES), jnp.bfloat16),
-                pltpu.VMEM((blocks * width, 1), jnp.float32),
+                pltpu.VMEM((blocks * width, LANES), jnp.float32),
                 pltpu.VMEM((blocks // 2, 1, 2 * LANES), jnp.float32),
             ],
         ),

time: 182 us -> 182 us (level)
  no operation moved by 1% of the time
where the time goes in v6:
time: 182 us
  blocking collectives  152 us (84%)
  Pallas kernels  28.4 us (16%)
    all_to_all x1, blocking collectives, on_device(): out = widen(lax.all_to_all(tiles, 'inp', 0, 0, tiled=True))  110 us
    all_to_all x1, blocking collectives, on_device(): turned = lax.all_to_all(spectra, EVERY, 0, 0, tiled=True)  41.8 us
    pallas_call x1, Pallas kernels, channelize(): pl.pallas_call(functools.partial(early_kernel, channels), name='channeliz...  10.3 us
    pallas_call x1, Pallas kernels, all_tiles(): pl.pallas_call(functools.partial(gram_kernel, float(frame_total)), name='...  8.22 us
    pallas_call x1, Pallas kernels, widen(): pl.pallas_call(widen_kernel, name='widen', in_specs=[pl.BlockSpec(memory_...  6.63 us
  transfers between devices with their start and end apart: 1, of which 0 were waited for; matrix products, arithmetic and copies ran while one was open for 0% of the time, Pallas kernels for 6%

profile of v6, /device:TPU:0, one launch (start us, length us, event | category | flops | bytes accessed | tf_op | source)
XLA Modules:
  0.0 181.9 jit_solution(15481034439935516673)
XLA Ops:
  0.0 1.1 halo.1
  1.1 1.3 collective-permute-start
  2.4 10.3 %channelize_early.1 = (bf16[1024,1024]{1,0:T(8,128)(2,1)S(1)}, bf16[1024,2048]{1,0:T(8,128)(2,1)S(1)}, f32[4,64,2048]{2,1,0:T(8,128)S(1)}, f32[4,2048]{1,0:T(4,128)S(1)}, s32[401]{0:T(512)S(1)}) custom-call(f32[64,128]{1,0:T(8,128)} %constant.6.clone.coarse_hbm, f32[64,1024]{1,0:T(8,128)} %constant.7.clone.fine_hbm, f32[4,2048]{1,0:T(4,128)} %constant.8.clone.window_hbm, ...), custom_call_target="tpu_custom_call" | custom-call | flops 3000000000 | bytes 12582912 | tf_op jit(solution)/shard_map/channelize_early/pallas_call | solution.py:230
  12.8 0.0 collective-permute-done.following
  12.8 2.1 %channelize_late.1 = bf16[1024,1024]{1,0:T(8,128)(2,1)S(1)} custom-call(bf16[1024,2048]{1,0:T(8,128)(2,1)S(1)} %get-tuple-element.11.table, f32[4,2048]{1,0:T(4,128)S(1)} %get-tuple-element.12.window, f32[4,64,2048]{2,1,0:T(8,128)S(1)} %get-tuple-element.13.partial, ...), custom_call_target="tpu_custom_call", output_to_operand_aliasing={{}: (4, {})} | custom-call | flops 1000000000 | bytes 6291456 | tf_op jit(solution)/shard_map/channelize_late/pallas_call | solution.py:255
  14.9 41.8 %all_to_all.10.spectra = bf16[128,8,1024]{2,1,0:T(8,128)(2,1)S(1)} all-to-all(bf16[128,8,1024]{2,1,0:T(8,128)(2,1)S(1)} %bitcast.5), channel_id=1, replica_groups=mesh['chan'=8,'inp'=16] {'chan','inp'}, dimensions={0} | all-to-all | bytes 4194304 | tf_op jit(solution)/shard_map/all_to_all | solution.py:426
  56.7 8.2 %gram.1 = bf16[576,64,128]{2,1,0:T(8,128)(2,1)S(1)} custom-call(s32[401]{0:T(512)S(1)} %get-tuple-element.10.places, bf16[128,8,1024]{2,1,0:T(8,128)(2,1)S(1)} %all_to_all.10.spectra), custom_call_target="tpu_custom_call" | custom-call | flops 3000000000 | bytes 12582912 | tf_op jit(solution)/shard_map/gram/pallas_call | solution.py:356
  65.0 110.3 %all_to_all.11.tiles = bf16[16,4,9,64,128]{4,3,2,1,0:T(8,128)(2,1)S(1)} all-to-all(bf16[16,4,9,64,128]{4,3,2,1,0:T(8,128)(2,1)S(1)} %bitcast.4), channel_id=1, replica_groups=mesh['chan'=8,'inp'=16] {'inp'}, dimensions={0} | all-to-all | bytes 18874368 | tf_op jit(solution)/shard_map/all_to_all | solution.py:429
  175.2 6.6 %widen.1 = f32[16,4,9,64,128]{4,3,2,1,0:T(8,128)} custom-call(bf16[16,4,9,64,128]{4,3,2,1,0:T(8,128)(2,1)S(1)} %all_to_all.11.tiles), custom_call_target="tpu_custom_call" | custom-call | bytes 29360128 | tf_op jit(solution)/shard_map/widen/pallas_call | solution.py:405
Async XLA Ops:
  1.1 11.7 %collective-permute-start = (bf16[64,6144]{1,0:T(8,128)(2,1)S(1)}, bf16[64,6144]{1,0:T(8,128)(2,1)S(1)}, u32[]{:S(2)}, u32[]{:S(2)}) collective-permute-start(bf16[64,6144]{1,0:T(8,128)(2,1)S(1)} %halo.1), channel_id=1, source_target_pairs={{16,0},{32,16},{48,32},{64,48},{80,64},{96,80},{112,96},{17,1},{33... | collective-permute-start | bytes 2359304 | tf_op jit(solution)/shard_map/ppermute | solution.py:223

commit v7 on v6

--- a/solution.py
+++ b/solution.py
@@ -122,8 +122,7 @@
     return empty
 
 
-def transform(table, filtered, spectra, columns, beside=None):
-    rows = 512
+def transform(table, filtered, spectra, columns, beside=None, rows=512):
     chunks = 2 * NCH // rows
     share = L // LANES // chunks
 
@@ -190,7 +189,7 @@
 
     lax.fori_loop(0, L // LANES, column, 0)
     first = spectra.shape[1] - filtered.shape[0]
-    transform(table, filtered, spectra, slice(first, spectra.shape[1]))
+    transform(table, filtered, spectra, slice(first, spectra.shape[1]), rows=2 * NCH)
 
 
 def halo_kernel(voltages, halo, sem):

time: 182 us -> 182 us (level)
  no operation moved by 1% of the time
where the time goes in v7:
time: 182 us
  blocking collectives  152 us (84%)
  Pallas kernels  28.2 us (15%)
    all_to_all x1, blocking collectives, on_device(): out = widen(lax.all_to_all(tiles, 'inp', 0, 0, tiled=True))  110 us
    all_to_all x1, blocking collectives, on_device(): turned = lax.all_to_all(spectra, EVERY, 0, 0, tiled=True)  41.8 us
    pallas_call x1, Pallas kernels, channelize(): pl.pallas_call(functools.partial(early_kernel, channels), name='channeliz...  10.3 us
    pallas_call x1, Pallas kernels, all_tiles(): pl.pallas_call(functools.partial(gram_kernel, float(frame_total)), name='...  8.21 us
    pallas_call x1, Pallas kernels, widen(): pl.pallas_call(widen_kernel, name='widen', in_specs=[pl.BlockSpec(memory_...  6.63 us
  transfers between devices with their start and end apart: 1, of which 0 were waited for; matrix products, arithmetic and copies ran while one was open for 0% of the time, Pallas kernels for 6%

profile of v7, /device:TPU:0, one launch (start us, length us, event | category | flops | bytes accessed | tf_op | source)
XLA Modules:
  0.0 181.6 jit_solution(17497506380212187564)
XLA Ops:
  0.0 1.1 halo.1
  1.1 1.3 collective-permute-start
  2.4 10.3 %channelize_early.1 = (bf16[1024,1024]{1,0:T(8,128)(2,1)S(1)}, bf16[1024,2048]{1,0:T(8,128)(2,1)S(1)}, f32[4,64,2048]{2,1,0:T(8,128)S(1)}, f32[4,2048]{1,0:T(4,128)S(1)}, s32[401]{0:T(512)S(1)}) custom-call(f32[64,128]{1,0:T(8,128)} %constant.6.clone.coarse_hbm, f32[64,1024]{1,0:T(8,128)} %constant.7.clone.fine_hbm, f32[4,2048]{1,0:T(4,128)} %constant.8.clone.window_hbm, ...), custom_call_target="tpu_custom_call" | custom-call | flops 3000000000 | bytes 12582912 | tf_op jit(solution)/shard_map/channelize_early/pallas_call | solution.py:229
  12.8 0.0 collective-permute-done.following
  12.8 1.9 %channelize_late.1 = bf16[1024,1024]{1,0:T(8,128)(2,1)S(1)} custom-call(bf16[1024,2048]{1,0:T(8,128)(2,1)S(1)} %get-tuple-element.11.table, f32[4,2048]{1,0:T(4,128)S(1)} %get-tuple-element.12.window, f32[4,64,2048]{2,1,0:T(8,128)S(1)} %get-tuple-element.13.partial, ...), custom_call_target="tpu_custom_call", output_to_operand_aliasing={{}: (4, {})} | custom-call | flops 1000000000 | bytes 6291456 | tf_op jit(solution)/shard_map/channelize_late/pallas_call | solution.py:254
  14.7 41.8 %all_to_all.10.spectra = bf16[128,8,1024]{2,1,0:T(8,128)(2,1)S(1)} all-to-all(bf16[128,8,1024]{2,1,0:T(8,128)(2,1)S(1)} %bitcast.5), channel_id=1, replica_groups=mesh['chan'=8,'inp'=16] {'chan','inp'}, dimensions={0} | all-to-all | bytes 4194304 | tf_op jit(solution)/shard_map/all_to_all | solution.py:425
  56.5 8.2 %gram.1 = bf16[576,64,128]{2,1,0:T(8,128)(2,1)S(1)} custom-call(s32[401]{0:T(512)S(1)} %get-tuple-element.10.places, bf16[128,8,1024]{2,1,0:T(8,128)(2,1)S(1)} %all_to_all.10.spectra), custom_call_target="tpu_custom_call" | custom-call | flops 3000000000 | bytes 12582912 | tf_op jit(solution)/shard_map/gram/pallas_call | solution.py:355
  64.8 110.3 %all_to_all.11.tiles = bf16[16,4,9,64,128]{4,3,2,1,0:T(8,128)(2,1)S(1)} all-to-all(bf16[16,4,9,64,128]{4,3,2,1,0:T(8,128)(2,1)S(1)} %bitcast.4), channel_id=1, replica_groups=mesh['chan'=8,'inp'=16] {'inp'}, dimensions={0} | all-to-all | bytes 18874368 | tf_op jit(solution)/shard_map/all_to_all | solution.py:428
  175.0 6.6 %widen.1 = f32[16,4,9,64,128]{4,3,2,1,0:T(8,128)} custom-call(bf16[16,4,9,64,128]{4,3,2,1,0:T(8,128)(2,1)S(1)} %all_to_all.11.tiles), custom_call_target="tpu_custom_call" | custom-call | bytes 29360128 | tf_op jit(solution)/shard_map/widen/pallas_call | solution.py:404
Async XLA Ops:
  1.1 11.7 %collective-permute-start = (bf16[64,6144]{1,0:T(8,128)(2,1)S(1)}, bf16[64,6144]{1,0:T(8,128)(2,1)S(1)}, u32[]{:S(2)}, u32[]{:S(2)}) collective-permute-start(bf16[64,6144]{1,0:T(8,128)(2,1)S(1)} %halo.1), channel_id=1, source_target_pairs={{16,0},{32,16},{48,32},{64,48},{80,64},{96,80},{112,96},{17,1},{33... | collective-permute-start | bytes 2359304 | tf_op jit(solution)/shard_map/ppermute | solution.py:222
